TPU v7x, 128 devices: a whole 4x4x4 slice. The times are simulated.
128 devices in a mesh: leaf: 8 (over x, core), tile: 16 (over y, z).
Axes of the slice: x: 4, y: 4, z: 4, core: 2. Of those that a mesh axis runs over, the one named last changes fastest.
Arguments:
- forcing_leaf: float32 [8, 4, 16, 64, 128], P('leaf', None, 'tile'), may hold values from -6 to 6
- inverse_leaf: float32 [8, 2, 16, 128, 128], P('leaf', None, 'tile'), may hold values from -0.2 to 2
- dense_leaf: float32 [8, 16, 32, 128, 128], P('leaf', 'tile'), may hold values from -0.25 to 0.25
- slot_leaf: int32 [8, 4, 16, 32], P('leaf', None, 'tile'), may hold values from -1 to 31, as said below
- left_leaf: float32 [8, 4, 16, 32, 32, 128], P('leaf', None, 'tile'), may hold values from -1 to 1
- right_leaf: float32 [8, 4, 16, 32, 32, 128], P('leaf', None, 'tile'), may hold values from -0.25 to 0.25
- rank_leaf: int32 [8, 4, 16, 32], P('leaf', None, 'tile'), may hold values from 1 to 32
- place_leaf: int32 [8, 2, 16], P('leaf', None, 'tile'), may hold values from 0 to 3, as said below
- forcing_root: float32 [4, 16, 64, 128], P(None, 'tile'), may hold values from -6 to 6
- inverse_root: float32 [2, 16, 128, 128], P(None, 'tile'), may hold values from -0.2 to 2
- dense_root: float32 [16, 32, 128, 128], P('tile'), may hold values from -0.25 to 0.25
- slot_root: int32 [4, 16, 32], P(None, 'tile'), may hold values from -1 to 31, as said below
- left_root: float32 [4, 16, 32, 32, 128], P(None, 'tile'), may hold values from -1 to 1
- right_root: float32 [4, 16, 32, 32, 128], P(None, 'tile'), may hold values from -0.25 to 0.25
- rank_root: int32 [4, 16, 32], P(None, 'tile'), may hold values from 1 to 32
Outputs:
- leaf_pivots: float32 [8, 2, 16, 64, 128], P('leaf', None, 'tile')
- root_pivots: float32 [2, 16, 64, 128], P(None, 'tile', 'leaf')
- root_updates: float32 [2, 16, 64, 128], P(None, 'tile', 'leaf')
Inputs may be any that keep to these rules, and one draw needn't show every extreme that they name: `slot_leaf`: in the 4 x 32 table of one leaf and one tile index, each of 0 to 31 appears exactly once and all other entries are -1. `slot_root`: in the 4 x 32 table of one tile index, each of 0 to 31 appears exactly once and all other entries are -1. `place_leaf`: the 2 entries of one leaf and one tile index are distinct.
All inputs are finite; a program needn't handle non-finite values.
Results may differ from a plain program's by a relative error of at most 0.0003.
Values sent between devices are 32-bit elements; how exact they have to be, the bound alone decides.
A program may use at most 64 MiB of HBM per device.

v0:
```python
import jax
import jax.numpy as jnp
from jax import lax
from jax.sharding import PartitionSpec as P

highest = lax.Precision.HIGHEST


def picked(shard, axis, root):
    return lax.dynamic_index_in_dim(lax.all_gather(shard, axis), root, 0, keepdims=False)


def cut_along(shard, dim, length):
    before, after = (shard.shape[:dim], shard.shape[dim + 1 :])
    return jnp.moveaxis(shard.reshape(*before, length, -1, *after), dim, 0)


def sum_at_owner(shard, axis, dim):
    blocks = cut_along(shard, dim, lax.axis_size(axis))
    arrived = lax.all_to_all(blocks, axis, split_axis=0, concat_axis=0, tiled=True)
    return arrived.sum(axis=0)


def apply_column(tile_set, slot_col, right_col, left_col, rank_col, solved):
    dense_out = jnp.einsum("lij,sj->lsi", tile_set, solved, precision=highest)
    projected = jnp.einsum("lrj,sj->lrs", right_col, solved, precision=highest)
    rank_mask = (
        jnp.arange(right_col.shape[1], dtype=jnp.int32)[None, :] < rank_col[:, None]
    ).astype(jnp.float32)
    low_out = jnp.einsum(
        "lri,lrs->lsi", left_col, projected * rank_mask[:, :, None], precision=highest
    )
    return jnp.where((slot_col >= 0)[:, None, None], dense_out, low_out)


def column_terms(column, solved, dense_pool, slot_map, left_fac, right_fac, rank_map):
    slot_col = lax.dynamic_index_in_dim(slot_map, column, 1, keepdims=False)
    rank_col = lax.dynamic_index_in_dim(rank_map, column, 1, keepdims=False)
    left_col = lax.dynamic_index_in_dim(left_fac, column, 1, keepdims=False)
    right_col = lax.dynamic_index_in_dim(right_fac, column, 1, keepdims=False)
    tile_set = dense_pool[jnp.maximum(slot_col, 0)]
    return apply_column(tile_set, slot_col, right_col, left_col, rank_col, solved)


def solve_block(column, rows_now, inverse, group_size):
    local_row = column // group_size
    pivot_in = lax.dynamic_index_in_dim(rows_now, local_row, 0, keepdims=False)
    inv_block = lax.dynamic_index_in_dim(inverse, local_row, 0, keepdims=False)
    solved = jnp.einsum("ab,sb->sa", inv_block, pivot_in, precision=highest)
    return picked(solved, "tile", column % group_size)


def solve_local(
    current, inverse, dense_pool, slot_map, left_fac, right_fac, rank_map, group_size, my_tile
):
    block_count = current.shape[0]
    pivot_blocks = slot_map.shape[1]
    row_ids = jnp.arange(block_count, dtype=jnp.int32) * group_size + my_tile

    def advance_all(column, rows_now):
        solved = solve_block(column, rows_now, inverse, group_size)
        update = column_terms(column, solved, dense_pool, slot_map, left_fac, right_fac, rank_map)
        rows_now = jnp.where((row_ids > column)[:, None, None], rows_now - update, rows_now)
        return jnp.where((row_ids == column)[:, None, None], solved[None], rows_now)

    return lax.fori_loop(0, pivot_blocks, advance_all, current)


def body(
    forcing_leaf,
    inverse_leaf,
    dense_leaf,
    slot_leaf,
    left_leaf,
    right_leaf,
    rank_leaf,
    place_leaf,
    forcing_root,
    inverse_root,
    dense_root,
    slot_root,
    left_root,
    right_root,
    rank_root,
):
    group_size = lax.axis_size("tile")
    leaf_count = lax.axis_size("leaf")
    my_tile = lax.axis_index("tile")
    my_leaf = lax.axis_index("leaf")
    pivot_count = inverse_leaf.shape[1]
    block_count = forcing_leaf.shape[1]
    leaf_out = solve_local(
        forcing_leaf[0, :, 0],
        inverse_leaf[0, :, 0],
        dense_leaf[0, 0],
        slot_leaf[0, :, 0],
        left_leaf[0, :, 0],
        right_leaf[0, :, 0],
        rank_leaf[0, :, 0],
        group_size,
        my_tile,
    )
    onehot = (
        place_leaf[0, :, 0][:, None] == jnp.arange(block_count, dtype=jnp.int32)[None, :]
    ).astype(jnp.float32)
    contrib = jnp.einsum("um,usb->msb", onehot, leaf_out[pivot_count:], precision=highest)
    sources = forcing_root.shape[2]
    share = sources // leaf_count
    summed = sum_at_owner(contrib, "leaf", 1)
    root_in = lax.dynamic_slice_in_dim(forcing_root[:, 0], my_leaf * share, share, 1) + summed
    root_out = solve_local(
        root_in,
        inverse_root[:, 0],
        dense_root[0],
        slot_root[:, 0],
        left_root[:, 0],
        right_root[:, 0],
        rank_root[:, 0],
        group_size,
        my_tile,
    )
    return (
        leaf_out[:pivot_count][None, :, None],
        root_out[:pivot_count][:, None],
        root_out[pivot_count:][:, None],
    )


def solution(mesh):
    placed = (
        P("leaf", None, "tile", None, None),
        P("leaf", None, "tile", None, None),
        P("leaf", "tile", None, None, None),
        P("leaf", None, "tile", None),
        P("leaf", None, "tile", None, None, None),
        P("leaf", None, "tile", None, None, None),
        P("leaf", None, "tile", None),
        P("leaf", None, "tile"),
        P(None, "tile", None, None),
        P(None, "tile", None, None),
        P("tile", None, None, None),
        P(None, "tile", None),
        P(None, "tile", None, None, None),
        P(None, "tile", None, None, None),
        P(None, "tile", None),
    )
    return jax.shard_map(
        body,
        mesh=mesh,
        in_specs=placed,
        out_specs=(
            P("leaf", None, "tile", None, None),
            P(None, "tile", "leaf", None),
            P(None, "tile", "leaf", None),
        ),
        check_vma=False,
    )
```

profile of v0, /device:TPU:0, one launch (start us, length us, event | category | flops | bytes accessed | tf_op | source)
XLA Modules:
  0.0 1736.5 jit_solution(3182493253238619792)
XLA Ops:
  4.1 870.3 %while.32 = (s32[]{:T(128)}, f32[4,64,128]{2,1,0:T(8,128)S(1)}, f32[2,128,128]{2,1,0:T(8,128)S(1)}, s32[4,32]{0,1:T(8,128)S(1)}, f32[32,128,128]{2,1,0:T(8,128)}...) while((s32[]{:T(128)}, f32[4,64,128]{2,1,0:T(8,128)S(1)}, ...), condition=%wide.region_1.2_spmd.clone, body=%wide.region_0.1_spmd.clone.sunk | while | flops 88220976 | bytes 2400805 | solution.py:66
  6.6 25.6 %all-gather.6 = f32[1024,128]{1,0:T(8,128)S(1)} all-gather(f32[64,128]{1,0:T(8,128)S(1)} %fusion.97), channel_id=2, replica_groups=mesh['leaf'=8,'tile'=16] {'tile'}, dimensions={0}, use_global_device_ids=true | all-gather | bytes 557056 | tf_op jit(solution)/shard_map/while/body/eval_jaxpr/all_gather | solution.py:10
  36.8 23.4 %all-gather.6 = f32[1024,128]{1,0:T(8,128)S(1)} all-gather(f32[64,128]{1,0:T(8,128)S(1)} %fusion.97), channel_id=2, replica_groups=mesh['leaf'=8,'tile'=16] {'tile'}, dimensions={0}, use_global_device_ids=true | all-gather | bytes 557056 | tf_op jit(solution)/shard_map/while/body/eval_jaxpr/all_gather | solution.py:10
  64.7 21.7 %all-gather.6 = f32[1024,128]{1,0:T(8,128)S(1)} all-gather(f32[64,128]{1,0:T(8,128)S(1)} %fusion.97), channel_id=2, replica_groups=mesh['leaf'=8,'tile'=16] {'tile'}, dimensions={0}, use_global_device_ids=true | all-gather | bytes 557056 | tf_op jit(solution)/shard_map/while/body/eval_jaxpr/all_gather | solution.py:10
  90.9 23.5 %all-gather.6 = f32[1024,128]{1,0:T(8,128)S(1)} all-gather(f32[64,128]{1,0:T(8,128)S(1)} %fusion.97), channel_id=2, replica_groups=mesh['leaf'=8,'tile'=16] {'tile'}, dimensions={0}, use_global_device_ids=true | all-gather | bytes 557056 | tf_op jit(solution)/shard_map/while/body/eval_jaxpr/all_gather | solution.py:10
  118.9 21.8 %all-gather.6 = f32[1024,128]{1,0:T(8,128)S(1)} all-gather(f32[64,128]{1,0:T(8,128)S(1)} %fusion.97), channel_id=2, replica_groups=mesh['leaf'=8,'tile'=16] {'tile'}, dimensions={0}, use_global_device_ids=true | all-gather | bytes 557056 | tf_op jit(solution)/shard_map/while/body/eval_jaxpr/all_gather | solution.py:10
  145.2 23.3 %all-gather.6 = f32[1024,128]{1,0:T(8,128)S(1)} all-gather(f32[64,128]{1,0:T(8,128)S(1)} %fusion.97), channel_id=2, replica_groups=mesh['leaf'=8,'tile'=16] {'tile'}, dimensions={0}, use_global_device_ids=true | all-gather | bytes 557056 | tf_op jit(solution)/shard_map/while/body/eval_jaxpr/all_gather | solution.py:10
  173.0 21.7 %all-gather.6 = f32[1024,128]{1,0:T(8,128)S(1)} all-gather(f32[64,128]{1,0:T(8,128)S(1)} %fusion.97), channel_id=2, replica_groups=mesh['leaf'=8,'tile'=16] {'tile'}, dimensions={0}, use_global_device_ids=true | all-gather | bytes 557056 | tf_op jit(solution)/shard_map/while/body/eval_jaxpr/all_gather | solution.py:10
  199.2 23.5 %all-gather.6 = f32[1024,128]{1,0:T(8,128)S(1)} all-gather(f32[64,128]{1,0:T(8,128)S(1)} %fusion.97), channel_id=2, replica_groups=mesh['leaf'=8,'tile'=16] {'tile'}, dimensions={0}, use_global_device_ids=true | all-gather | bytes 557056 | tf_op jit(solution)/shard_map/while/body/eval_jaxpr/all_gather | solution.py:10
  227.2 21.8 %all-gather.6 = f32[1024,128]{1,0:T(8,128)S(1)} all-gather(f32[64,128]{1,0:T(8,128)S(1)} %fusion.97), channel_id=2, replica_groups=mesh['leaf'=8,'tile'=16] {'tile'}, dimensions={0}, use_global_device_ids=true | all-gather | bytes 557056 | tf_op jit(solution)/shard_map/while/body/eval_jaxpr/all_gather | solution.py:10
  253.5 23.2 %all-gather.6 = f32[1024,128]{1,0:T(8,128)S(1)} all-gather(f32[64,128]{1,0:T(8,128)S(1)} %fusion.97), channel_id=2, replica_groups=mesh['leaf'=8,'tile'=16] {'tile'}, dimensions={0}, use_global_device_ids=true | all-gather | bytes 557056 | tf_op jit(solution)/shard_map/while/body/eval_jaxpr/all_gather | solution.py:10
  281.3 21.9 %all-gather.6 = f32[1024,128]{1,0:T(8,128)S(1)} all-gather(f32[64,128]{1,0:T(8,128)S(1)} %fusion.97), channel_id=2, replica_groups=mesh['leaf'=8,'tile'=16] {'tile'}, dimensions={0}, use_global_device_ids=true | all-gather | bytes 557056 | tf_op jit(solution)/shard_map/while/body/eval_jaxpr/all_gather | solution.py:10
  307.6 23.3 %all-gather.6 = f32[1024,128]{1,0:T(8,128)S(1)} all-gather(f32[64,128]{1,0:T(8,128)S(1)} %fusion.97), channel_id=2, replica_groups=mesh['leaf'=8,'tile'=16] {'tile'}, dimensions={0}, use_global_device_ids=true | all-gather | bytes 557056 | tf_op jit(solution)/shard_map/while/body/eval_jaxpr/all_gather | solution.py:10
  335.4 22.0 %all-gather.6 = f32[1024,128]{1,0:T(8,128)S(1)} all-gather(f32[64,128]{1,0:T(8,128)S(1)} %fusion.97), channel_id=2, replica_groups=mesh['leaf'=8,'tile'=16] {'tile'}, dimensions={0}, use_global_device_ids=true | all-gather | bytes 557056 | tf_op jit(solution)/shard_map/while/body/eval_jaxpr/all_gather | solution.py:10
  361.9 23.1 %all-gather.6 = f32[1024,128]{1,0:T(8,128)S(1)} all-gather(f32[64,128]{1,0:T(8,128)S(1)} %fusion.97), channel_id=2, replica_groups=mesh['leaf'=8,'tile'=16] {'tile'}, dimensions={0}, use_global_device_ids=true | all-gather | bytes 557056 | tf_op jit(solution)/shard_map/while/body/eval_jaxpr/all_gather | solution.py:10
  389.5 22.0 %all-gather.6 = f32[1024,128]{1,0:T(8,128)S(1)} all-gather(f32[64,128]{1,0:T(8,128)S(1)} %fusion.97), channel_id=2, replica_groups=mesh['leaf'=8,'tile'=16] {'tile'}, dimensions={0}, use_global_device_ids=true | all-gather | bytes 557056 | tf_op jit(solution)/shard_map/while/body/eval_jaxpr/all_gather | solution.py:10
  416.0 23.4 %all-gather.6 = f32[1024,128]{1,0:T(8,128)S(1)} all-gather(f32[64,128]{1,0:T(8,128)S(1)} %fusion.97), channel_id=2, replica_groups=mesh['leaf'=8,'tile'=16] {'tile'}, dimensions={0}, use_global_device_ids=true | all-gather | bytes 557056 | tf_op jit(solution)/shard_map/while/body/eval_jaxpr/all_gather | solution.py:10
  443.9 21.7 %all-gather.6 = f32[1024,128]{1,0:T(8,128)S(1)} all-gather(f32[64,128]{1,0:T(8,128)S(1)} %fusion.97), channel_id=2, replica_groups=mesh['leaf'=8,'tile'=16] {'tile'}, dimensions={0}, use_global_device_ids=true | all-gather | bytes 557056 | tf_op jit(solution)/shard_map/while/body/eval_jaxpr/all_gather | solution.py:10
  470.1 23.3 %all-gather.6 = f32[1024,128]{1,0:T(8,128)S(1)} all-gather(f32[64,128]{1,0:T(8,128)S(1)} %fusion.97), channel_id=2, replica_groups=mesh['leaf'=8,'tile'=16] {'tile'}, dimensions={0}, use_global_device_ids=true | all-gather | bytes 557056 | tf_op jit(solution)/shard_map/while/body/eval_jaxpr/all_gather | solution.py:10
  497.9 21.8 %all-gather.6 = f32[1024,128]{1,0:T(8,128)S(1)} all-gather(f32[64,128]{1,0:T(8,128)S(1)} %fusion.97), channel_id=2, replica_groups=mesh['leaf'=8,'tile'=16] {'tile'}, dimensions={0}, use_global_device_ids=true | all-gather | bytes 557056 | tf_op jit(solution)/shard_map/while/body/eval_jaxpr/all_gather | solution.py:10
  524.2 23.3 %all-gather.6 = f32[1024,128]{1,0:T(8,128)S(1)} all-gather(f32[64,128]{1,0:T(8,128)S(1)} %fusion.97), channel_id=2, replica_groups=mesh['leaf'=8,'tile'=16] {'tile'}, dimensions={0}, use_global_device_ids=true | all-gather | bytes 557056 | tf_op jit(solution)/shard_map/while/body/eval_jaxpr/all_gather | solution.py:10
  552.0 22.1 %all-gather.6 = f32[1024,128]{1,0:T(8,128)S(1)} all-gather(f32[64,128]{1,0:T(8,128)S(1)} %fusion.97), channel_id=2, replica_groups=mesh['leaf'=8,'tile'=16] {'tile'}, dimensions={0}, use_global_device_ids=true | all-gather | bytes 557056 | tf_op jit(solution)/shard_map/while/body/eval_jaxpr/all_gather | solution.py:10
  578.6 23.4 %all-gather.6 = f32[1024,128]{1,0:T(8,128)S(1)} all-gather(f32[64,128]{1,0:T(8,128)S(1)} %fusion.97), channel_id=2, replica_groups=mesh['leaf'=8,'tile'=16] {'tile'}, dimensions={0}, use_global_device_ids=true | all-gather | bytes 557056 | tf_op jit(solution)/shard_map/while/body/eval_jaxpr/all_gather | solution.py:10
  606.5 21.7 %all-gather.6 = f32[1024,128]{1,0:T(8,128)S(1)} all-gather(f32[64,128]{1,0:T(8,128)S(1)} %fusion.97), channel_id=2, replica_groups=mesh['leaf'=8,'tile'=16] {'tile'}, dimensions={0}, use_global_device_ids=true | all-gather | bytes 557056 | tf_op jit(solution)/shard_map/while/body/eval_jaxpr/all_gather | solution.py:10
  632.7 23.3 %all-gather.6 = f32[1024,128]{1,0:T(8,128)S(1)} all-gather(f32[64,128]{1,0:T(8,128)S(1)} %fusion.97), channel_id=2, replica_groups=mesh['leaf'=8,'tile'=16] {'tile'}, dimensions={0}, use_global_device_ids=true | all-gather | bytes 557056 | tf_op jit(solution)/shard_map/while/body/eval_jaxpr/all_gather | solution.py:10
  660.5 22.1 %all-gather.6 = f32[1024,128]{1,0:T(8,128)S(1)} all-gather(f32[64,128]{1,0:T(8,128)S(1)} %fusion.97), channel_id=2, replica_groups=mesh['leaf'=8,'tile'=16] {'tile'}, dimensions={0}, use_global_device_ids=true | all-gather | bytes 557056 | tf_op jit(solution)/shard_map/while/body/eval_jaxpr/all_gather | solution.py:10
  687.1 23.2 %all-gather.6 = f32[1024,128]{1,0:T(8,128)S(1)} all-gather(f32[64,128]{1,0:T(8,128)S(1)} %fusion.97), channel_id=2, replica_groups=mesh['leaf'=8,'tile'=16] {'tile'}, dimensions={0}, use_global_device_ids=true | all-gather | bytes 557056 | tf_op jit(solution)/shard_map/while/body/eval_jaxpr/all_gather | solution.py:10
  714.8 21.9 %all-gather.6 = f32[1024,128]{1,0:T(8,128)S(1)} all-gather(f32[64,128]{1,0:T(8,128)S(1)} %fusion.97), channel_id=2, replica_groups=mesh['leaf'=8,'tile'=16] {'tile'}, dimensions={0}, use_global_device_ids=true | all-gather | bytes 557056 | tf_op jit(solution)/shard_map/while/body/eval_jaxpr/all_gather | solution.py:10
  741.2 23.1 %all-gather.6 = f32[1024,128]{1,0:T(8,128)S(1)} all-gather(f32[64,128]{1,0:T(8,128)S(1)} %fusion.97), channel_id=2, replica_groups=mesh['leaf'=8,'tile'=16] {'tile'}, dimensions={0}, use_global_device_ids=true | all-gather | bytes 557056 | tf_op jit(solution)/shard_map/while/body/eval_jaxpr/all_gather | solution.py:10
  768.8 21.9 %all-gather.6 = f32[1024,128]{1,0:T(8,128)S(1)} all-gather(f32[64,128]{1,0:T(8,128)S(1)} %fusion.97), channel_id=2, replica_groups=mesh['leaf'=8,'tile'=16] {'tile'}, dimensions={0}, use_global_device_ids=true | all-gather | bytes 557056 | tf_op jit(solution)/shard_map/while/body/eval_jaxpr/all_gather | solution.py:10
  795.2 23.1 %all-gather.6 = f32[1024,128]{1,0:T(8,128)S(1)} all-gather(f32[64,128]{1,0:T(8,128)S(1)} %fusion.97), channel_id=2, replica_groups=mesh['leaf'=8,'tile'=16] {'tile'}, dimensions={0}, use_global_device_ids=true | all-gather | bytes 557056 | tf_op jit(solution)/shard_map/while/body/eval_jaxpr/all_gather | solution.py:10
  822.9 21.9 %all-gather.6 = f32[1024,128]{1,0:T(8,128)S(1)} all-gather(f32[64,128]{1,0:T(8,128)S(1)} %fusion.97), channel_id=2, replica_groups=mesh['leaf'=8,'tile'=16] {'tile'}, dimensions={0}, use_global_device_ids=true | all-gather | bytes 557056 | tf_op jit(solution)/shard_map/while/body/eval_jaxpr/all_gather | solution.py:10
  849.3 23.1 %all-gather.6 = f32[1024,128]{1,0:T(8,128)S(1)} all-gather(f32[64,128]{1,0:T(8,128)S(1)} %fusion.97), channel_id=2, replica_groups=mesh['leaf'=8,'tile'=16] {'tile'}, dimensions={0}, use_global_device_ids=true | all-gather | bytes 557056 | tf_op jit(solution)/shard_map/while/body/eval_jaxpr/all_gather | solution.py:10
  886.0 849.9 %while.33 = (s32[]{:T(128)}, f32[4,8,128]{2,1,0:T(8,128)S(1)}, f32[2,128,128]{2,1,0:T(8,128)S(1)}, s32[4,32]{0,1:T(8,128)S(1)}, f32[32,128,128]{2,1,0:T(8,128)},...) while((s32[]{:T(128)}, f32[4,8,128]{2,1,0:T(8,128)S(1)}, ...), condition=%wide.region_4.5_spmd.clone, body=%wide.region_3.4_spmd.clone.sunk | while | flops 11028782 | bytes 1176101 | solution.py:66
  914.1 23.2 %all-gather.7 = f32[128,128]{1,0:T(8,128)S(1)} all-gather(f32[8,128]{1,0:T(8,128)S(1)} %fusion.110), channel_id=3, replica_groups=mesh['leaf'=8,'tile'=16] {'tile'}, dimensions={0}, use_global_device_ids=true | all-gather | bytes 69632 | tf_op jit(solution)/shard_map/while/body/eval_jaxpr/all_gather | solution.py:10
  967.2 23.2 %all-gather.7 = f32[128,128]{1,0:T(8,128)S(1)} all-gather(f32[8,128]{1,0:T(8,128)S(1)} %fusion.110), channel_id=3, replica_groups=mesh['leaf'=8,'tile'=16] {'tile'}, dimensions={0}, use_global_device_ids=true | all-gather | bytes 69632 | tf_op jit(solution)/shard_map/while/body/eval_jaxpr/all_gather | solution.py:10
  994.7 21.4 %all-gather.7 = f32[128,128]{1,0:T(8,128)S(1)} all-gather(f32[8,128]{1,0:T(8,128)S(1)} %fusion.110), channel_id=3, replica_groups=mesh['leaf'=8,'tile'=16] {'tile'}, dimensions={0}, use_global_device_ids=true | all-gather | bytes 69632 | tf_op jit(solution)/shard_map/while/body/eval_jaxpr/all_gather | solution.py:10
  1020.4 23.2 %all-gather.7 = f32[128,128]{1,0:T(8,128)S(1)} all-gather(f32[8,128]{1,0:T(8,128)S(1)} %fusion.110), channel_id=3, replica_groups=mesh['leaf'=8,'tile'=16] {'tile'}, dimensions={0}, use_global_device_ids=true | all-gather | bytes 69632 | tf_op jit(solution)/shard_map/while/body/eval_jaxpr/all_gather | solution.py:10
  1047.8 21.4 %all-gather.7 = f32[128,128]{1,0:T(8,128)S(1)} all-gather(f32[8,128]{1,0:T(8,128)S(1)} %fusion.110), channel_id=3, replica_groups=mesh['leaf'=8,'tile'=16] {'tile'}, dimensions={0}, use_global_device_ids=true | all-gather | bytes 69632 | tf_op jit(solution)/shard_map/while/body/eval_jaxpr/all_gather | solution.py:10
  1073.5 23.2 %all-gather.7 = f32[128,128]{1,0:T(8,128)S(1)} all-gather(f32[8,128]{1,0:T(8,128)S(1)} %fusion.110), channel_id=3, replica_groups=mesh['leaf'=8,'tile'=16] {'tile'}, dimensions={0}, use_global_device_ids=true | all-gather | bytes 69632 | tf_op jit(solution)/shard_map/while/body/eval_jaxpr/all_gather | solution.py:10
  1100.9 21.5 %all-gather.7 = f32[128,128]{1,0:T(8,128)S(1)} all-gather(f32[8,128]{1,0:T(8,128)S(1)} %fusion.110), channel_id=3, replica_groups=mesh['leaf'=8,'tile'=16] {'tile'}, dimensions={0}, use_global_device_ids=true | all-gather | bytes 69632 | tf_op jit(solution)/shard_map/while/body/eval_jaxpr/all_gather | solution.py:10
  1126.6 23.1 %all-gather.7 = f32[128,128]{1,0:T(8,128)S(1)} all-gather(f32[8,128]{1,0:T(8,128)S(1)} %fusion.110), channel_id=3, replica_groups=mesh['leaf'=8,'tile'=16] {'tile'}, dimensions={0}, use_global_device_ids=true | all-gather | bytes 69632 | tf_op jit(solution)/shard_map/while/body/eval_jaxpr/all_gather | solution.py:10
  1154.0 21.5 %all-gather.7 = f32[128,128]{1,0:T(8,128)S(1)} all-gather(f32[8,128]{1,0:T(8,128)S(1)} %fusion.110), channel_id=3, replica_groups=mesh['leaf'=8,'tile'=16] {'tile'}, dimensions={0}, use_global_device_ids=true | all-gather | bytes 69632 | tf_op jit(solution)/shard_map/while/body/eval_jaxpr/all_gather | solution.py:10
  1179.7 23.1 %all-gather.7 = f32[128,128]{1,0:T(8,128)S(1)} all-gather(f32[8,128]{1,0:T(8,128)S(1)} %fusion.110), channel_id=3, replica_groups=mesh['leaf'=8,'tile'=16] {'tile'}, dimensions={0}, use_global_device_ids=true | all-gather | bytes 69632 | tf_op jit(solution)/shard_map/while/body/eval_jaxpr/all_gather | solution.py:10
  1207.1 21.6 %all-gather.7 = f32[128,128]{1,0:T(8,128)S(1)} all-gather(f32[8,128]{1,0:T(8,128)S(1)} %fusion.110), channel_id=3, replica_groups=mesh['leaf'=8,'tile'=16] {'tile'}, dimensions={0}, use_global_device_ids=true | all-gather | bytes 69632 | tf_op jit(solution)/shard_map/while/body/eval_jaxpr/all_gather | solution.py:10
  1232.9 23.1 %all-gather.7 = f32[128,128]{1,0:T(8,128)S(1)} all-gather(f32[8,128]{1,0:T(8,128)S(1)} %fusion.110), channel_id=3, replica_groups=mesh['leaf'=8,'tile'=16] {'tile'}, dimensions={0}, use_global_device_ids=true | all-gather | bytes 69632 | tf_op jit(solution)/shard_map/while/body/eval_jaxpr/all_gather | solution.py:10
  1260.2 21.6 %all-gather.7 = f32[128,128]{1,0:T(8,128)S(1)} all-gather(f32[8,128]{1,0:T(8,128)S(1)} %fusion.110), channel_id=3, replica_groups=mesh['leaf'=8,'tile'=16] {'tile'}, dimensions={0}, use_global_device_ids=true | all-gather | bytes 69632 | tf_op jit(solution)/shard_map/while/body/eval_jaxpr/all_gather | solution.py:10
  1286.0 23.1 %all-gather.7 = f32[128,128]{1,0:T(8,128)S(1)} all-gather(f32[8,128]{1,0:T(8,128)S(1)} %fusion.110), channel_id=3, replica_groups=mesh['leaf'=8,'tile'=16] {'tile'}, dimensions={0}, use_global_device_ids=true | all-gather | bytes 69632 | tf_op jit(solution)/shard_map/while/body/eval_jaxpr/all_gather | solution.py:10
  1313.4 21.5 %all-gather.7 = f32[128,128]{1,0:T(8,128)S(1)} all-gather(f32[8,128]{1,0:T(8,128)S(1)} %fusion.110), channel_id=3, replica_groups=mesh['leaf'=8,'tile'=16] {'tile'}, dimensions={0}, use_global_device_ids=true | all-gather | bytes 69632 | tf_op jit(solution)/shard_map/while/body/eval_jaxpr/all_gather | solution.py:10
  1339.1 23.1 %all-gather.7 = f32[128,128]{1,0:T(8,128)S(1)} all-gather(f32[8,128]{1,0:T(8,128)S(1)} %fusion.110), channel_id=3, replica_groups=mesh['leaf'=8,'tile'=16] {'tile'}, dimensions={0}, use_global_device_ids=true | all-gather | bytes 69632 | tf_op jit(solution)/shard_map/while/body/eval_jaxpr/all_gather | solution.py:10
  1366.5 21.5 %all-gather.7 = f32[128,128]{1,0:T(8,128)S(1)} all-gather(f32[8,128]{1,0:T(8,128)S(1)} %fusion.110), channel_id=3, replica_groups=mesh['leaf'=8,'tile'=16] {'tile'}, dimensions={0}, use_global_device_ids=true | all-gather | bytes 69632 | tf_op jit(solution)/shard_map/while/body/eval_jaxpr/all_gather | solution.py:10
  1392.3 23.1 %all-gather.7 = f32[128,128]{1,0:T(8,128)S(1)} all-gather(f32[8,128]{1,0:T(8,128)S(1)} %fusion.110), channel_id=3, replica_groups=mesh['leaf'=8,'tile'=16] {'tile'}, dimensions={0}, use_global_device_ids=true | all-gather | bytes 69632 | tf_op jit(solution)/shard_map/while/body/eval_jaxpr/all_gather | solution.py:10
  1419.6 21.5 %all-gather.7 = f32[128,128]{1,0:T(8,128)S(1)} all-gather(f32[8,128]{1,0:T(8,128)S(1)} %fusion.110), channel_id=3, replica_groups=mesh['leaf'=8,'tile'=16] {'tile'}, dimensions={0}, use_global_device_ids=true | all-gather | bytes 69632 | tf_op jit(solution)/shard_map/while/body/eval_jaxpr/all_gather | solution.py:10
  1445.4 23.1 %all-gather.7 = f32[128,128]{1,0:T(8,128)S(1)} all-gather(f32[8,128]{1,0:T(8,128)S(1)} %fusion.110), channel_id=3, replica_groups=mesh['leaf'=8,'tile'=16] {'tile'}, dimensions={0}, use_global_device_ids=true | all-gather | bytes 69632 | tf_op jit(solution)/shard_map/while/body/eval_jaxpr/all_gather | solution.py:10
  1472.7 21.5 %all-gather.7 = f32[128,128]{1,0:T(8,128)S(1)} all-gather(f32[8,128]{1,0:T(8,128)S(1)} %fusion.110), channel_id=3, replica_groups=mesh['leaf'=8,'tile'=16] {'tile'}, dimensions={0}, use_global_device_ids=true | all-gather | bytes 69632 | tf_op jit(solution)/shard_map/while/body/eval_jaxpr/all_gather | solution.py:10
  1498.5 23.1 %all-gather.7 = f32[128,128]{1,0:T(8,128)S(1)} all-gather(f32[8,128]{1,0:T(8,128)S(1)} %fusion.110), channel_id=3, replica_groups=mesh['leaf'=8,'tile'=16] {'tile'}, dimensions={0}, use_global_device_ids=true | all-gather | bytes 69632 | tf_op jit(solution)/shard_map/while/body/eval_jaxpr/all_gather | solution.py:10
  1525.9 21.5 %all-gather.7 = f32[128,128]{1,0:T(8,128)S(1)} all-gather(f32[8,128]{1,0:T(8,128)S(1)} %fusion.110), channel_id=3, replica_groups=mesh['leaf'=8,'tile'=16] {'tile'}, dimensions={0}, use_global_device_ids=true | all-gather | bytes 69632 | tf_op jit(solution)/shard_map/while/body/eval_jaxpr/all_gather | solution.py:10
  1551.6 23.1 %all-gather.7 = f32[128,128]{1,0:T(8,128)S(1)} all-gather(f32[8,128]{1,0:T(8,128)S(1)} %fusion.110), channel_id=3, replica_groups=mesh['leaf'=8,'tile'=16] {'tile'}, dimensions={0}, use_global_device_ids=true | all-gather | bytes 69632 | tf_op jit(solution)/shard_map/while/body/eval_jaxpr/all_gather | solution.py:10
  1579.0 21.5 %all-gather.7 = f32[128,128]{1,0:T(8,128)S(1)} all-gather(f32[8,128]{1,0:T(8,128)S(1)} %fusion.110), channel_id=3, replica_groups=mesh['leaf'=8,'tile'=16] {'tile'}, dimensions={0}, use_global_device_ids=true | all-gather | bytes 69632 | tf_op jit(solution)/shard_map/while/body/eval_jaxpr/all_gather | solution.py:10
  1604.7 23.1 %all-gather.7 = f32[128,128]{1,0:T(8,128)S(1)} all-gather(f32[8,128]{1,0:T(8,128)S(1)} %fusion.110), channel_id=3, replica_groups=mesh['leaf'=8,'tile'=16] {'tile'}, dimensions={0}, use_global_device_ids=true | all-gather | bytes 69632 | tf_op jit(solution)/shard_map/while/body/eval_jaxpr/all_gather | solution.py:10
  1632.1 21.5 %all-gather.7 = f32[128,128]{1,0:T(8,128)S(1)} all-gather(f32[8,128]{1,0:T(8,128)S(1)} %fusion.110), channel_id=3, replica_groups=mesh['leaf'=8,'tile'=16] {'tile'}, dimensions={0}, use_global_device_ids=true | all-gather | bytes 69632 | tf_op jit(solution)/shard_map/while/body/eval_jaxpr/all_gather | solution.py:10
  1657.8 23.1 %all-gather.7 = f32[128,128]{1,0:T(8,128)S(1)} all-gather(f32[8,128]{1,0:T(8,128)S(1)} %fusion.110), channel_id=3, replica_groups=mesh['leaf'=8,'tile'=16] {'tile'}, dimensions={0}, use_global_device_ids=true | all-gather | bytes 69632 | tf_op jit(solution)/shard_map/while/body/eval_jaxpr/all_gather | solution.py:10
  1685.2 21.5 %all-gather.7 = f32[128,128]{1,0:T(8,128)S(1)} all-gather(f32[8,128]{1,0:T(8,128)S(1)} %fusion.110), channel_id=3, replica_groups=mesh['leaf'=8,'tile'=16] {'tile'}, dimensions={0}, use_global_device_ids=true | all-gather | bytes 69632 | tf_op jit(solution)/shard_map/while/body/eval_jaxpr/all_gather | solution.py:10
  1710.9 23.1 %all-gather.7 = f32[128,128]{1,0:T(8,128)S(1)} all-gather(f32[8,128]{1,0:T(8,128)S(1)} %fusion.110), channel_id=3, replica_groups=mesh['leaf'=8,'tile'=16] {'tile'}, dimensions={0}, use_global_device_ids=true | all-gather | bytes 69632 | tf_op jit(solution)/shard_map/while/body/eval_jaxpr/all_gather | solution.py:10
  (736 shorter events, 331.9 us)
Async XLA Ops:
  0.6 881.9 %copy-start = (f32[4,1,64,128]{3,2,1,0:T(8,128)S(1)}, f32[4,1,64,128]{3,2,1,0:T(8,128)}, u32[]{:S(2)}) copy-start(f32[4,1,64,128]{3,2,1,0:T(8,128)} %param.27) | copy-start | bytes 393220
  2.2 1.9 copy-start.1
  2.2 1.9 copy-start.2
  4.1 870.4 %copy-start.6 = (s32[1,2,1]{1,2,0:T(1,128)S(1)}, s32[1,2,1]{1,2,0:T(1,128)}, u32[]{:S(2)}) copy-start(s32[1,2,1]{1,2,0:T(1,128)} %param.26) | copy-start | bytes 28
  4.1 876.4 %copy-start.4 = (s32[4,1,32]{2,1,0:T(1,128)S(1)}, s32[4,1,32]{2,1,0:T(1,128)}, u32[]{:S(2)}) copy-start(s32[4,1,32]{2,1,0:T(1,128)} %param.30) | copy-start | bytes 1540
  4.1 876.5 %copy-start.5 = (s32[4,1,32]{2,1,0:T(1,128)S(1)}, s32[4,1,32]{2,1,0:T(1,128)}, u32[]{:S(2)}) copy-start(s32[4,1,32]{2,1,0:T(1,128)} %param.33) | copy-start | bytes 1540
  875.5 10.4 all-to-all-start
  880.7 5.3 copy-start.3
where the time goes:
time: 1740 us
  blocking collectives  1440 us (83%)
  local copies, waits for them, and re-layouts  145 us (8%)
  matrix products  128 us (7%)
    all_gather x64, blocking collectives, picked(): lax.all_gather(shard, axis)  1440 us
    gather x64, local copies, waits for them, and re-layouts, column_terms(): tile_set = dense_pool[jnp.maximum(slot_col, 0)]  138 us
    dot_general x64, matrix products, apply_column(): projected = jnp.einsum('lrj,sj->lrs', right_col, solved, precision=highest)  72.2 us
  transfers between devices with their start and end apart: 1, of which 1 were waited for; matrix products, arithmetic and copies ran while one was open for 0% of the time, Pallas kernels for 0%

commit v1 on v0

v1 whole, which is shorter than its diff:
```python
import functools

import jax
import jax.numpy as jnp
from jax import lax
from jax.experimental import pallas as pl
from jax.experimental.pallas import tpu as pltpu
from jax.sharding import PartitionSpec as P

F32 = jnp.float32
BF16 = jnp.bfloat16
MESH = pl.DeviceIdType.MESH


def split(a):
    high = a.astype(BF16)
    return high, (a - high.astype(F32)).astype(BF16)


def dot_nn(a, b):
    return lax.dot_general(a, b, (((1,), (0,)), ((), ())), preferred_element_type=F32)


def dot_nt(a, b):
    return lax.dot_general(a, b, (((1,), (1,)), ((), ())), preferred_element_type=F32)


def mul_nn(a, b):
    ah, al = split(a)
    bh, bl = split(b)
    return dot_nn(jnp.concatenate([ah, al], 1), jnp.concatenate([bh, bh], 0)) + dot_nn(ah, bl)


def mul_nt(x, wh, wl):
    rows = x.shape[0]
    xh = x.astype(BF16)
    xhf = xh.astype(F32)
    both = jnp.concatenate([xhf, x - xhf], 0).astype(BF16)
    first = dot_nt(both, wh)
    return first[:rows] + first[rows:] + dot_nt(xh, wl)


class Front:
    def __init__(self, **refs):
        self.__dict__.update(refs)

    def masked_right(self, l, k):
        right = self.right[l, k]
        row = lax.broadcasted_iota(jnp.int32, right.shape, 0)
        return jnp.where(row < self.rank[0, l, 0, k], right, 0.0)

    def choose(self, l, k, low):
        slot = self.slot[0, l, 0, k]
        dense = self.dense[jnp.maximum(slot, 0)]
        return jnp.where(slot >= 0, dense, low)

    def tile(self, l, k):
        left = self.left[l, k]
        lh = left.astype(BF16).astype(F32)
        rh, rl = split(self.masked_right(l, k))
        zero = jnp.zeros_like(left)
        cols = jnp.concatenate([lh, left - lh, lh, zero], 0).T.astype(BF16)
        rows = jnp.concatenate([rh, rh, rl, zero.astype(BF16)], 0)
        return self.choose(l, k, dot_nn(cols, rows))

    def prepare_column(self, pair, half):
        k = 2 * pair + half
        blocks = self.left.shape[0]
        lt = jnp.concatenate([self.left[l, k] for l in range(blocks)], 0).T
        lh, ll = split(lt)
        rights = [split(self.masked_right(l, k)) for l in range(blocks)]

        def diagonal(part):
            zero = jnp.zeros_like(rights[0][0])
            return jnp.concatenate(
                [
                    jnp.concatenate([rights[l][part] if m == l else zero for m in range(blocks)], 1)
                    for l in range(blocks)
                ],
                0,
            )

        rh, rl = diagonal(0), diagonal(1)
        low = dot_nn(jnp.concatenate([lh, ll], 1), jnp.concatenate([rh, rh], 0)) + dot_nn(lh, rl)
        for l in range(blocks):
            th, tl = split(self.choose(l, k, low[:, 128 * l : 128 * (l + 1)]))
            self.wh[pair, 128 * l : 128 * (l + 1), 128 * half : 128 * (half + 1)] = th
            self.wl[pair, 128 * l : 128 * (l + 1), 128 * half : 128 * (half + 1)] = tl

    def prepare(self, pair):
        self.prepare_column(pair, 0)
        self.prepare_column(pair, 1)

    def send_x(self, l, me, to, order):
        i = l * self.tiles + me
        return pltpu.make_async_remote_copy(
            self.x.at[i], self.x.at[i], self.xs.at[l, order], self.xr.at[i],
            device_id={"tile": to}, device_id_type=MESH,
        )

    def wait_x(self, i):
        pltpu.make_async_remote_copy(
            self.x.at[i], self.x.at[i], self.xs.at[0, 0], self.xr.at[i],
            device_id={"tile": 0}, device_id_type=MESH,
        ).wait_recv()

    def copy_c(self, l, to):
        return pltpu.make_async_remote_copy(
            self.c.at[l], self.cin.at[l], self.cs.at[l], self.cr.at[l],
            device_id={"tile": to}, device_id_type=MESH,
        )

    def copy_p(self, l, to):
        return pltpu.make_async_remote_copy(
            self.pout.at[l], self.pin.at[l], self.ps.at[l], self.pr.at[l],
            device_id={"tile": to}, device_id_type=MESH,
        )

    def previous(self, l, me):
        return jnp.maximum(l * (self.tiles // 2) + me // 2 - 1, 0)

    def start_p(self, l, me):
        prev = self.previous(l, me)
        for half in range(2):
            part = mul_nn(self.inverse[l], self.tile(l, 2 * prev + half))
            cols = slice(128 * half, 128 * (half + 1))
            self.pout[l, :, cols] = part
            self.ph[l, :, cols], self.pl[l, :, cols] = split(part)
        self.copy_p(l, me + 1).start()

    def own_b(self, l, me):
        group = l * (self.tiles // 2) + me // 2
        part = mul_nn(self.inverse[l], self.tile(l, 2 * group))
        self.bmat[l] = part
        self.bh[l], self.bl[l] = split(part)

    def finish_p(self, l, me):
        prev = self.previous(l, me)
        parts = [mul_nn(self.inverse[l], self.tile(l, 2 * prev + half)) for half in range(2)]
        self.copy_p(l, me).wait_recv()
        for half in range(2):
            cols = slice(128 * half, 128 * (half + 1))
            part = parts[half] - mul_nn(self.bmat[l], self.pin[l, :, cols])
            self.ph[l, :, cols], self.pl[l, :, cols] = split(part)

    def start_c(self, l, me):
        dh, dl = split(self.inverse[l])
        self.c[l] = mul_nt(self.b[l], dh, dl)

        @pl.when(me % 2 == 0)
        def _():
            self.copy_c(l, me + 1).start()

    def finish_c(self, l, me):
        self.copy_c(l, me).wait_recv()
        self.c[l] = self.c[l] - mul_nt(self.cin[l], self.bh[l], self.bl[l])

    def emit(self, l, me, solved):
        i = l * self.tiles + me
        self.x[i] = solved
        for order, step in enumerate(self.steps):
            self.send_x(l, me, lax.rem(me + step, self.tiles), order).start()

    def arrive(self, pair, me):
        @pl.when(me // 2 != lax.rem(pair, self.groups))
        def _():
            self.wait_x(2 * pair)
            self.wait_x(2 * pair + 1)

        @pl.when(me // 2 == lax.rem(pair, self.groups))
        def _():
            self.wait_x(2 * pair + 1 - me % 2)

    def pair_now(self, pair):
        return jnp.concatenate([self.x[2 * pair], self.x[2 * pair + 1]], 1)

    def update(self, pair, me):
        out = mul_nt(self.pair_now(pair), self.wh[pair], self.wl[pair])
        for l in range(self.b.shape[0]):
            part = out[:, 128 * l : 128 * (l + 1)]
            if l < 2:
                later = (l * self.groups + me // 2 > pair + 1).astype(F32)
                part = part * later
            self.b[l] = self.b[l] - part

    def wait_sends(self, me):
        for l in range(2):
            for order, step in enumerate(self.steps):
                self.send_x(l, me, lax.rem(me + step, self.tiles), order).wait_send()

        @pl.when(me % 2 == 0)
        def _():
            for l in range(2):
                self.copy_c(l, me + 1).wait_send()
                self.copy_p(l, me + 1).wait_send()


def first_steps(front, me):
    @pl.when(me // 2 < 2)
    def _():
        front.start_c(0, me)

    @pl.when(me == 1)
    def _():
        front.finish_c(0, me)

    @pl.when(me // 2 == 0)
    def _():
        front.emit(0, me, front.c[0])


def run_front(front, me, extra):
    pairs = 2 * front.groups

    def step(pair, carry):
        extra(pair)
        mine_next = jnp.logical_and(pair + 1 < pairs, me // 2 == lax.rem(pair + 1, front.groups))
        mine_then = jnp.logical_and(pair + 2 < pairs, me // 2 == lax.rem(pair + 2, front.groups))
        l_next = lax.rem(pair + 1, pairs) // front.groups
        l_then = lax.rem(pair + 2, pairs) // front.groups

        @pl.when(jnp.logical_and(mine_next, me % 2 == 1))
        def _():
            front.finish_c(l_next, me)

        front.arrive(pair, me)

        @pl.when(mine_next)
        def _():
            solved = mul_nt(front.pair_now(pair), front.ph[l_next], front.pl[l_next])
            front.emit(l_next, me, front.c[l_next] - solved)

        front.update(pair, me)

        @pl.when(mine_then)
        def _():
            front.start_c(l_then, me)

        return carry

    lax.fori_loop(0, pairs, step, 0)


def kernel(sizes, *refs):
    tiles, leaves, blocks, sources = sizes
    share = sources // leaves
    names_in = ("forcing", "inverse", "dense", "slot", "left", "right", "rank")
    leaf_in = dict(zip(names_in, refs[:7]))
    place = refs[7]
    root_in = dict(zip(names_in, refs[8:15]))
    leaf_pivots, root_pivots, root_updates = refs[15:18]
    scratch = list(refs[18:])
    me = lax.axis_index("tile")
    my_leaf = lax.axis_index("leaf")
    order = [2, 1, 3] + [s for s in range(4, tiles)]
    order = [s for s in order if s < tiles]
    if tiles - 1 in order[3:]:
        order.remove(tiles - 1)
        order.insert(4, tiles - 1)

    def front_of(inputs):
        names = (
            "b", "x", "c", "cin", "pout", "pin", "ph", "pl", "bmat", "bh", "bl", "wh", "wl",
            "inverse", "dense", "left", "right",
            "xs", "xr", "cs", "cr", "ps", "pr", "load",
        )
        mine = {name: scratch.pop(0) for name in names}
        return Front(
            slot=inputs["slot"], rank=inputs["rank"], tiles=tiles, groups=tiles // 2,
            steps=order, **mine,
        )

    leaf = front_of(leaf_in)
    root = front_of(root_in)
    root_forcing, sum_out, sum_in, sum_send, sum_recv = scratch

    def load(front, inputs, forcing):
        pairs = [(inputs["forcing"], forcing)] + [
            (inputs[n], getattr(front, n)) for n in ("inverse", "left", "right", "dense")
        ]
        return [
            pltpu.make_async_copy(src, dst, front.load.at[n]) for n, (src, dst) in enumerate(pairs)
        ]

    leaf_loads = load(leaf, leaf_in, leaf.b)
    root_loads = load(root, root_in, root_forcing)
    for copy in leaf_loads:
        copy.start()
    for copy in root_loads:
        copy.start()

    barrier = pltpu.get_barrier_semaphore()
    for step in range(1, tiles):
        pl.semaphore_signal(
            barrier, inc=1, device_id={"tile": lax.rem(me + step, tiles)}, device_id_type=MESH
        )
    for step in range(1, leaves):
        pl.semaphore_signal(
            barrier, inc=1, device_id={"leaf": lax.rem(my_leaf + step, leaves)}, device_id_type=MESH
        )
    for copy in leaf_loads:
        copy.wait()
    pl.semaphore_wait(barrier, tiles + leaves - 2)

    odd = me % 2 == 1
    even = me % 2 == 0

    def setup_first(front):
        @pl.when(even)
        def _():
            front.start_p(0, me)
            front.start_p(1, me)

        @pl.when(odd)
        def _():
            front.own_b(0, me)
            front.own_b(1, me)

    def setup_last(front):
        @pl.when(odd)
        def _():
            front.finish_p(0, me)
            front.finish_p(1, me)

    @pl.when(odd)
    def _():
        leaf.own_b(0, me)

    first_steps(leaf, me)

    @pl.when(even)
    def _():
        leaf.start_p(0, me)
        leaf.start_p(1, me)

    @pl.when(odd)
    def _():
        leaf.own_b(1, me)

    setup_last(leaf)
    for copy in root_loads:
        copy.wait()

    def beside(pair):
        leaf.prepare(pair)
        root.prepare(pair)

        @pl.when(pair == 1)
        def _():
            setup_first(root)

        @pl.when(pair == tiles - 2)
        def _():
            setup_last(root)

    run_front(leaf, me, beside)

    for l in range(2):
        leaf_pivots[l] = leaf.x[l * tiles + me]

    for m in range(blocks):
        part = jnp.zeros((sources, 128), F32)
        for u in range(2):
            part = part + leaf.b[2 + u] * (place[0, u, 0] == m).astype(F32)
        for g in range(leaves):
            sum_out[g, m] = part[share * g : share * (g + 1)]

    def sum_copy(step, there):
        return pltpu.make_async_remote_copy(
            sum_out.at[there], sum_in.at[my_leaf], sum_send.at[step], sum_recv.at[my_leaf],
            device_id={"leaf": there}, device_id_type=MESH,
        )

    def sum_wait(here):
        return pltpu.make_async_remote_copy(
            sum_out.at[here], sum_in.at[here], sum_send.at[0], sum_recv.at[here],
            device_id={"leaf": here}, device_id_type=MESH,
        )

    for step in range(1, leaves):
        sum_copy(step, lax.rem(my_leaf + step, leaves)).start()
    for m in range(blocks):
        mine = root_forcing[m, pl.ds(pl.multiple_of(my_leaf * share, share), share)]
        root.b[m] = mine + sum_out[my_leaf, m]
    for step in range(1, leaves):
        here = lax.rem(my_leaf + step, leaves)
        sum_wait(here).wait_recv()
        for m in range(blocks):
            root.b[m] = root.b[m] + sum_in[here, m]

    first_steps(root, me)
    run_front(root, me, lambda pair: None)
    for l in range(2):
        root_pivots[l] = root.x[l * tiles + me]
        root_updates[l] = root.b[2 + l]

    leaf.wait_sends(me)
    root.wait_sends(me)
    for step in range(1, leaves):
        sum_copy(step, lax.rem(my_leaf + step, leaves)).wait_send()


def front_scratch(tiles, blocks, sources, dense_count, rank):
    pivots = 2 * tiles
    pairs = tiles
    blk = 128
    vmem = pltpu.VMEM
    dma = pltpu.SemaphoreType.DMA
    return [
        vmem((blocks, sources, blk), F32),
        vmem((pivots, sources, blk), F32),
        vmem((2, sources, blk), F32),
        vmem((2, sources, blk), F32),
        vmem((2, blk, 2 * blk), F32),
        vmem((2, blk, 2 * blk), F32),
        vmem((2, blk, 2 * blk), BF16),
        vmem((2, blk, 2 * blk), BF16),
        vmem((2, blk, blk), F32),
        vmem((2, blk, blk), BF16),
        vmem((2, blk, blk), BF16),
        vmem((pairs, blocks * blk, 2 * blk), BF16),
        vmem((pairs, blocks * blk, 2 * blk), BF16),
        vmem((2, blk, blk), F32),
        vmem((dense_count, blk, blk), F32),
        vmem((blocks, pivots, rank, blk), F32),
        vmem((blocks, pivots, rank, blk), F32),
        dma((2, tiles - 1)),
        dma((pivots,)),
        dma((2,)),
        dma((2,)),
        dma((2,)),
        dma((2,)),
        dma((5,)),
    ]


def body(
    forcing_leaf,
    inverse_leaf,
    dense_leaf,
    slot_leaf,
    left_leaf,
    right_leaf,
    rank_leaf,
    place_leaf,
    forcing_root,
    inverse_root,
    dense_root,
    slot_root,
    left_root,
    right_root,
    rank_root,
):
    tiles = lax.axis_size("tile")
    leaves = lax.axis_size("leaf")
    blocks, sources, blk = forcing_leaf.shape[1], forcing_leaf.shape[3], forcing_leaf.shape[4]
    dense_count, rank = dense_leaf.shape[2], left_leaf.shape[4]
    share = sources // leaves
    args = (
        forcing_leaf[0, :, 0],
        inverse_leaf[0, :, 0],
        dense_leaf[0, 0],
        slot_leaf,
        left_leaf[0, :, 0],
        right_leaf[0, :, 0],
        rank_leaf,
        place_leaf,
        forcing_root[:, 0],
        inverse_root[:, 0],
        dense_root[0],
        slot_root[None],
        left_root[:, 0],
        right_root[:, 0],
        rank_root[None],
    )
    smem = pl.BlockSpec(memory_space=pltpu.SMEM)
    hbm = pl.BlockSpec(memory_space=pl.ANY)
    vmem = pl.BlockSpec(memory_space=pltpu.VMEM)
    one = [hbm, hbm, hbm, smem, hbm, hbm, smem]
    leaf_pivots, root_pivots, root_updates = pl.pallas_call(
        functools.partial(kernel, (tiles, leaves, blocks, sources)),
        out_shape=(
            jax.ShapeDtypeStruct((2, sources, blk), F32),
            jax.ShapeDtypeStruct((2, share, blk), F32),
            jax.ShapeDtypeStruct((2, share, blk), F32),
        ),
        in_specs=one + [smem] + one,
        out_specs=(vmem, vmem, vmem),
        scratch_shapes=front_scratch(tiles, blocks, sources, dense_count, rank)
        + front_scratch(tiles, blocks, share, dense_count, rank)
        + [
            pltpu.VMEM((blocks, sources, blk), F32),
            pltpu.VMEM((leaves, blocks, share, blk), F32),
            pltpu.VMEM((leaves, blocks, share, blk), F32),
            pltpu.SemaphoreType.DMA((leaves,)),
            pltpu.SemaphoreType.DMA((leaves,)),
        ],
        compiler_params=pltpu.CompilerParams(
            collective_id=0, has_side_effects=True, vmem_limit_bytes=60 * 2**20
        ),
    )(*args)
    return leaf_pivots[None, :, None], root_pivots[:, None], root_updates[:, None]


def solution(mesh):
    placed = (
        P("leaf", None, "tile", None, None),
        P("leaf", None, "tile", None, None),
        P("leaf", "tile", None, None, None),
        P("leaf", None, "tile", None),
        P("leaf", None, "tile", None, None, None),
        P("leaf", None, "tile", None, None, None),
        P("leaf", None, "tile", None),
        P("leaf", None, "tile"),
        P(None, "tile", None, None),
        P(None, "tile", None, None),
        P("tile", None, None, None),
        P(None, "tile", None),
        P(None, "tile", None, None, None),
        P(None, "tile", None, None, None),
        P(None, "tile", None),
    )
    return jax.shard_map(
        body,
        mesh=mesh,
        in_specs=placed,
        out_specs=(
            P("leaf", None, "tile", None, None),
            P(None, "tile", "leaf", None),
            P(None, "tile", "leaf", None),
        ),
        check_vma=False,
    )
```

time: 1740 us -> 161 us (0.09)
  blocking collectives: 1440 us -> 0 us
  Pallas kernels: 0 us -> 155 us
  local copies, waits for them, and re-layouts: 145 us -> 5.36 us
  matrix products: 128 us -> 0 us
    all_gather x64 -> x0, blocking collectives: 1440 us -> none  [picked(): lax.all_gather(shard, axis)]
    pallas_call x0 -> x1, Pallas kernels: none -> 155 us  [body(): pl.pallas_call(functools.partial(kernel, (tiles, leaves, blocks, sources)...]
    gather x64 -> x0, local copies, waits for them, and re-layouts: 138 us -> none  [column_terms(): tile_set = dense_pool[jnp.maximum(slot_col, 0)]]
    dot_general x257 -> x0, matrix products: 128 us -> none  [the longest x64 72.2 us: apply_column(): projected = jnp.einsum('lrj,sj->lrs', right_col, solved, precision=highest)]
  transfers between devices with their start and end apart: 1 -> 0, of which waited for: 1 -> 0; matrix products, arithmetic and copies ran while one was open for 0% -> 0% of each run, Pallas kernels for 0% -> 0%
where the time goes in v1:
time: 161 us
  Pallas kernels  155 us (96%)
  local copies, waits for them, and re-layouts  5.36 us (3%)
    pallas_call x1, Pallas kernels, body(): pl.pallas_call(functools.partial(kernel, (tiles, leaves, blocks, sources)...  155 us
    unnamed x4, local copies, waits for them, and re-layouts  5.36 us

profile of v1, /device:TPU:0, one launch (start us, length us, event | category | flops | bytes accessed | tf_op | source)
XLA Modules:
  0.0 161.1 jit_solution(6341932233263447172)
XLA Ops:
  0.6 1.3 copy.18.refs_7_
  1.9 155.1 %shard_map.166 = (f32[2,64,128]{2,1,0:T(8,128)}, f32[2,8,128]{2,1,0:T(8,128)}, f32[2,8,128]{2,1,0:T(8,128)}) custom-call(f32[4,64,128]{2,1,0:T(8,128)} %bitcast.31, f32[2,128,128]{2,1,0:T(8,128)} %bitcast.32, f32[32,128,128]{2,1,0:T(8,128)} %bitcast.25, s32[1,4,1,32]{3,2,1,0:T(1,128)} %refs_3_.1, f32[4,32,32,128]{3,2,1,0:T(8,128)} %bitcast.26, ...), custom_call_target="tpu_custom_call" | custom-call | tf_op jit(solution)/shard_map/pallas_call | solution.py:480
  157.0 1.5 copy.27
  158.5 1.3 copy.28
  159.8 1.3 copy.29

commit v2 on v1

--- a/solution.py
+++ b/solution.py
@@ -193,6 +193,186 @@
             for l in range(2):
                 self.copy_c(l, me + 1).wait_send()
                 self.copy_p(l, me + 1).wait_send()
+
+
+SPAN = 4
+
+
+class Root(Front):
+    def place(self, me):
+        return me // SPAN, lax.rem(me, SPAN)
+
+    def z_tile(self, l, q, to, back):
+        return pltpu.make_async_remote_copy(
+            self.zall.at[l, self.my_leaf], self.zin.at[l, q], self.zs.at[l, back], self.zr.at[l, q],
+            device_id={"tile": to}, device_id_type=MESH,
+        )
+
+    def z_leaf(self, l, step):
+        there = lax.rem(self.my_leaf + step, self.leaves)
+        return pltpu.make_async_remote_copy(
+            self.zall.at[l, self.my_leaf], self.zall.at[l, self.my_leaf],
+            self.gs.at[l, step], self.gr.at[l, self.my_leaf],
+            device_id={"leaf": there}, device_id_type=MESH,
+        )
+
+    def solve_z(self, l, me):
+        y, q = self.place(me)
+        group = l * self.groups + y
+        column = SPAN * jnp.maximum(group - 1, 0) + jnp.minimum(self.my_leaf, SPAN - 1)
+        shape = (128, 128)
+        same = lax.broadcasted_iota(jnp.int32, shape, 0) == lax.broadcasted_iota(jnp.int32, shape, 1)
+        unit = same.astype(F32) * (self.my_leaf - SPAN == q).astype(F32)
+        self.zwork[...] = jnp.where(self.my_leaf < SPAN, self.tile(l, column), unit)
+        for before in range(SPAN - 1):
+            @pl.when(before < q)
+            def _(before=before):
+                inner = self.tile(l, SPAN * group + before)
+                self.z_tile(l, before, me, 0).wait_recv()
+                self.zwork[...] = self.zwork[...] - mul_nn(inner, self.zin[l, before])
+
+        self.zall[l, self.my_leaf] = mul_nn(self.inverse[l], self.zwork[...])
+        for step in range(1, SPAN):
+            @pl.when(q + step < SPAN)
+            def _(step=step):
+                self.z_tile(l, q, me + step, step).start()
+
+        for step in range(1, self.leaves):
+            self.z_leaf(l, step).start()
+
+    def take_z(self, l):
+        for g in range(2 * SPAN):
+            @pl.when(self.my_leaf != g)
+            def _(g=g):
+                pltpu.make_async_remote_copy(
+                    self.zall.at[l, g], self.zall.at[l, g], self.gs.at[l, 0], self.gr.at[l, g],
+                    device_id={"leaf": 0}, device_id_type=MESH,
+                ).wait_recv()
+
+            at = slice(128 * (g % SPAN), 128 * (g % SPAN + 1))
+            if g < SPAN:
+                self.ph[l, :, at], self.pl[l, :, at] = split(self.zall[l, g])
+            else:
+                self.gh[l, :, at], self.gl[l, :, at] = split(self.zall[l, g])
+
+    def clear(self, me):
+        q = lax.rem(me, SPAN)
+        for l in range(2):
+            for other in range(SPAN):
+                @pl.when(other > q)
+                def _(l=l, other=other):
+                    self.bin[l, other] = jnp.zeros_like(self.bin[l, other])
+
+    def routes(self, me):
+        y, q = self.place(me)
+        for down in [1, 0] + list(range(2, self.groups)):
+            for right in (2, 1, 3, 0):
+                if down % self.groups or right:
+                    to = lax.rem(y + down, self.groups) * SPAN + lax.rem(q + right, SPAN)
+                    yield (down % self.groups) * SPAN + right, to
+
+    def emit(self, l, me, solved):
+        self.x[l * self.tiles + me] = solved
+        for order, to in self.routes(me):
+            self.send_x(l, me, to, order).start()
+
+    def copy_b(self, l, q, to, step):
+        return pltpu.make_async_remote_copy(
+            self.bin.at[l, q], self.bin.at[l, q], self.bs.at[l, step], self.br.at[l, q],
+            device_id={"tile": to}, device_id_type=MESH,
+        )
+
+    def start_c(self, l, me):
+        q = lax.rem(me, SPAN)
+        self.bin[l, q] = self.b[l]
+        for step in range(1, SPAN):
+            @pl.when(q + step < SPAN)
+            def _(step=step):
+                self.copy_b(l, q, me + step, step).start()
+
+    def finish_c(self, l, me):
+        q = lax.rem(me, SPAN)
+        for before in range(SPAN - 1):
+            @pl.when(before < q)
+            def _(before=before):
+                self.copy_b(l, before, me, 0).wait_recv()
+
+        whole = jnp.concatenate([self.bin[l, other] for other in range(SPAN)], 1)
+        self.c[l] = mul_nt(whole, self.gh[l], self.gl[l])
+
+    def arrive(self, group, me):
+        for n in range(SPAN):
+            i = SPAN * group + n
+            @pl.when(me != lax.rem(i, self.tiles))
+            def _(i=i):
+                self.wait_x(i)
+
+    def group_now(self, group):
+        return jnp.concatenate([self.x[SPAN * group + n] for n in range(SPAN)], 1)
+
+    def update(self, group, me):
+        now = self.group_now(group)
+        out = mul_nt(now[:, :256], self.wh[2 * group], self.wl[2 * group])
+        out = out + mul_nt(now[:, 256:], self.wh[2 * group + 1], self.wl[2 * group + 1])
+        for l in range(self.b.shape[0]):
+            part = out[:, 128 * l : 128 * (l + 1)]
+            if l < 2:
+                part = part * (l * self.groups + me // SPAN > group + 1).astype(F32)
+            self.b[l] = self.b[l] - part
+
+    def run(self, me):
+        groups = 2 * self.groups
+        y = me // SPAN
+
+        @pl.when(y < 2)
+        def _():
+            self.start_c(0, me)
+
+        @pl.when(y == 0)
+        def _():
+            self.finish_c(0, me)
+            self.emit(0, me, self.c[0])
+
+        def step(group, carry):
+            mine_next = jnp.logical_and(group + 1 < groups, y == lax.rem(group + 1, self.groups))
+            mine_then = jnp.logical_and(group + 2 < groups, y == lax.rem(group + 2, self.groups))
+            l_next = lax.rem(group + 1, groups) // self.groups
+            l_then = lax.rem(group + 2, groups) // self.groups
+
+            @pl.when(mine_next)
+            def _():
+                self.finish_c(l_next, me)
+
+            self.arrive(group, me)
+
+            @pl.when(mine_next)
+            def _():
+                solved = mul_nt(self.group_now(group), self.ph[l_next], self.pl[l_next])
+                self.emit(l_next, me, self.c[l_next] - solved)
+
+            self.update(group, me)
+
+            @pl.when(mine_then)
+            def _():
+                self.start_c(l_then, me)
+
+            return carry
+
+        lax.fori_loop(0, groups, step, 0)
+
+    def wait_sends(self, me):
+        y, q = self.place(me)
+        for l in range(2):
+            for order, to in self.routes(me):
+                self.send_x(l, me, to, order).wait_send()
+            for step in range(1, SPAN):
+                @pl.when(q + step < SPAN)
+                def _(l=l, step=step):
+                    self.copy_b(l, q, me + step, step).wait_send()
+                    self.z_tile(l, q, me + step, step).wait_send()
+
+            for step in range(1, self.leaves):
+                self.z_leaf(l, step).wait_send()
 
 
 def first_steps(front, me):
@@ -258,20 +438,24 @@
         order.remove(tiles - 1)
         order.insert(4, tiles - 1)
 
-    def front_of(inputs):
-        names = (
-            "b", "x", "c", "cin", "pout", "pin", "ph", "pl", "bmat", "bh", "bl", "wh", "wl",
-            "inverse", "dense", "left", "right",
-            "xs", "xr", "cs", "cr", "ps", "pr", "load",
-        )
+    common = (
+        "b", "x", "c", "wh", "wl", "inverse", "dense", "left", "right", "xs", "xr", "load", "ph", "pl",
+    )
+    for_leaf = ("cin", "pout", "pin", "bmat", "bh", "bl", "cs", "cr", "ps", "pr")
+    for_root = (
+        "gh", "gl", "bin", "zin", "zall", "zwork", "zs", "zr", "gs", "gr", "bs", "br",
+    )
+
+    def front_of(kind, inputs, names, groups, **more):
         mine = {name: scratch.pop(0) for name in names}
-        return Front(
-            slot=inputs["slot"], rank=inputs["rank"], tiles=tiles, groups=tiles // 2,
-            steps=order, **mine,
-        )
-
-    leaf = front_of(leaf_in)
-    root = front_of(root_in)
+        return kind(
+            slot=inputs["slot"], rank=inputs["rank"], tiles=tiles, groups=groups, **more, **mine
+        )
+
+    leaf = front_of(Front, leaf_in, common + for_leaf, tiles // 2, steps=order)
+    root = front_of(
+        Root, root_in, common + for_root, tiles // SPAN, leaves=leaves, my_leaf=my_leaf
+    )
     root_forcing, sum_out, sum_in, sum_send, sum_recv = scratch
 
     def load(front, inputs, forcing):
@@ -305,23 +489,6 @@
     odd = me % 2 == 1
     even = me % 2 == 0
 
-    def setup_first(front):
-        @pl.when(even)
-        def _():
-            front.start_p(0, me)
-            front.start_p(1, me)
-
-        @pl.when(odd)
-        def _():
-            front.own_b(0, me)
-            front.own_b(1, me)
-
-    def setup_last(front):
-        @pl.when(odd)
-        def _():
-            front.finish_p(0, me)
-            front.finish_p(1, me)
-
     @pl.when(odd)
     def _():
         leaf.own_b(0, me)
@@ -337,7 +504,12 @@
     def _():
         leaf.own_b(1, me)
 
-    setup_last(leaf)
+    @pl.when(odd)
+    def _():
+        leaf.finish_p(0, me)
+        leaf.finish_p(1, me)
+
+    root.clear(me)
     for copy in root_loads:
         copy.wait()
 
@@ -345,13 +517,15 @@
         leaf.prepare(pair)
         root.prepare(pair)
 
-        @pl.when(pair == 1)
-        def _():
-            setup_first(root)
-
-        @pl.when(pair == tiles - 2)
-        def _():
-            setup_last(root)
+        @pl.when(pair == 1 + 2 * lax.rem(me, SPAN))
+        def _():
+            root.solve_z(0, me)
+            root.solve_z(1, me)
+
+        @pl.when(pair == tiles - 3)
+        def _():
+            root.take_z(0)
+            root.take_z(1)
 
     run_front(leaf, me, beside)
 
@@ -388,8 +562,7 @@
         for m in range(blocks):
             root.b[m] = root.b[m] + sum_in[here, m]
 
-    first_steps(root, me)
-    run_front(root, me, lambda pair: None)
+    root.run(me)
     for l in range(2):
         root_pivots[l] = root.x[l * tiles + me]
         root_updates[l] = root.b[2 + l]
@@ -400,9 +573,8 @@
         sum_copy(step, lax.rem(my_leaf + step, leaves)).wait_send()
 
 
-def front_scratch(tiles, blocks, sources, dense_count, rank):
+def common_scratch(tiles, blocks, sources, dense_count, rank, span):
     pivots = 2 * tiles
-    pairs = tiles
     blk = 128
     vmem = pltpu.VMEM
     dma = pltpu.SemaphoreType.DMA
@@ -410,27 +582,55 @@
         vmem((blocks, sources, blk), F32),
         vmem((pivots, sources, blk), F32),
         vmem((2, sources, blk), F32),
-        vmem((2, sources, blk), F32),
-        vmem((2, blk, 2 * blk), F32),
-        vmem((2, blk, 2 * blk), F32),
-        vmem((2, blk, 2 * blk), BF16),
-        vmem((2, blk, 2 * blk), BF16),
-        vmem((2, blk, blk), F32),
-        vmem((2, blk, blk), BF16),
-        vmem((2, blk, blk), BF16),
-        vmem((pairs, blocks * blk, 2 * blk), BF16),
-        vmem((pairs, blocks * blk, 2 * blk), BF16),
+        vmem((tiles, blocks * blk, 2 * blk), BF16),
+        vmem((tiles, blocks * blk, 2 * blk), BF16),
         vmem((2, blk, blk), F32),
         vmem((dense_count, blk, blk), F32),
         vmem((blocks, pivots, rank, blk), F32),
         vmem((blocks, pivots, rank, blk), F32),
-        dma((2, tiles - 1)),
+        dma((2, tiles)),
         dma((pivots,)),
+        dma((5,)),
+        vmem((2, blk, span * blk), BF16),
+        vmem((2, blk, span * blk), BF16),
+    ]
+
+
+def leaf_scratch(sources):
+    blk = 128
+    vmem = pltpu.VMEM
+    dma = pltpu.SemaphoreType.DMA
+    return [
+        vmem((2, sources, blk), F32),
+        vmem((2, blk, 2 * blk), F32),
+        vmem((2, blk, 2 * blk), F32),
+        vmem((2, blk, blk), F32),
+        vmem((2, blk, blk), BF16),
+        vmem((2, blk, blk), BF16),
         dma((2,)),
         dma((2,)),
         dma((2,)),
         dma((2,)),
-        dma((5,)),
+    ]
+
+
+def root_scratch(sources, leaves):
+    blk = 128
+    vmem = pltpu.VMEM
+    dma = pltpu.SemaphoreType.DMA
+    return [
+        vmem((2, blk, SPAN * blk), BF16),
+        vmem((2, blk, SPAN * blk), BF16),
+        vmem((2, SPAN, sources, blk), F32),
+        vmem((2, SPAN, blk, blk), F32),
+        vmem((2, leaves, blk, blk), F32),
+        vmem((blk, blk), F32),
+        dma((2, SPAN)),
+        dma((2, SPAN)),
+        dma((2, leaves)),
+        dma((2, leaves)),
+        dma((2, SPAN)),
+        dma((2, SPAN)),
     ]
 
 
@@ -486,8 +686,10 @@
         ),
         in_specs=one + [smem] + one,
         out_specs=(vmem, vmem, vmem),
-        scratch_shapes=front_scratch(tiles, blocks, sources, dense_count, rank)
-        + front_scratch(tiles, blocks, share, dense_count, rank)
+        scratch_shapes=common_scratch(tiles, blocks, sources, dense_count, rank, 2)
+        + leaf_scratch(sources)
+        + common_scratch(tiles, blocks, share, dense_count, rank, SPAN)
+        + root_scratch(share, leaves)
         + [
             pltpu.VMEM((blocks, sources, blk), F32),
             pltpu.VMEM((leaves, blocks, share, blk), F32),

time: 161 us -> 137 us (0.85)
  Pallas kernels: 155 us -> 131 us
    pallas_call x1, Pallas kernels: 155 us -> 131 us  [body(): pl.pallas_call(functools.partial(kernel, (tiles, leaves, blocks, sources)...]
where the time goes in v2:
time: 137 us
  Pallas kernels  131 us (96%)
  local copies, waits for them, and re-layouts  5.36 us (4%)
    pallas_call x1, Pallas kernels, body(): pl.pallas_call(functools.partial(kernel, (tiles, leaves, blocks, sources)...  131 us
    unnamed x4, local copies, waits for them, and re-layouts  5.36 us

profile of v2, /device:TPU:0, one launch (start us, length us, event | category | flops | bytes accessed | tf_op | source)
XLA Modules:
  0.0 136.6 jit_solution(422720963283577240)
XLA Ops:
  0.6 1.3 copy.18.refs_7_
  1.9 130.6 %shard_map.166 = (f32[2,64,128]{2,1,0:T(8,128)}, f32[2,8,128]{2,1,0:T(8,128)}, f32[2,8,128]{2,1,0:T(8,128)}) custom-call(f32[4,64,128]{2,1,0:T(8,128)} %bitcast.31, f32[2,128,128]{2,1,0:T(8,128)} %bitcast.32, f32[32,128,128]{2,1,0:T(8,128)} %bitcast.25, s32[1,4,1,32]{3,2,1,0:T(1,128)} %refs_3_.1, f32[4,32,32,128]{3,2,1,0:T(8,128)} %bitcast.26, ...), custom_call_target="tpu_custom_call" | custom-call | tf_op jit(solution)/shard_map/pallas_call | solution.py:680
  132.6 1.5 %copy.27 = f32[1,2,1,64,128]{4,3,2,1,0:T(8,128)} copy(f32[1,2,1,64,128]{4,3,2,1,0:T(8,128)} %bitcast.35) | data formatting | bytes 131072
  134.0 1.3 copy.28
  135.3 1.3 copy.29

commit v3 on v2

v3 whole, which is shorter than its diff:
```python
import functools

import jax
import jax.numpy as jnp
from jax import lax
from jax.experimental import pallas as pl
from jax.experimental.pallas import tpu as pltpu
from jax.sharding import PartitionSpec as P

F32 = jnp.float32
BF16 = jnp.bfloat16
MESH = pl.DeviceIdType.MESH


def split(a):
    high = a.astype(BF16)
    return high, (a - high.astype(F32)).astype(BF16)


def dot_nn(a, b):
    return lax.dot_general(a, b, (((1,), (0,)), ((), ())), preferred_element_type=F32)


def dot_nt(a, b):
    return lax.dot_general(a, b, (((1,), (1,)), ((), ())), preferred_element_type=F32)


def mul_nn(a, b):
    ah, al = split(a)
    bh, bl = split(b)
    return dot_nn(jnp.concatenate([ah, al], 1), jnp.concatenate([bh, bh], 0)) + dot_nn(ah, bl)


def mul_nt(x, wh, wl):
    rows = x.shape[0]
    xh = x.astype(BF16)
    xhf = xh.astype(F32)
    both = jnp.concatenate([xhf, x - xhf], 0).astype(BF16)
    first = dot_nt(both, wh)
    return first[:rows] + first[rows:] + dot_nt(xh, wl)


class Front:
    def __init__(self, **refs):
        self.__dict__.update(refs)

    def masked_right(self, l, k):
        right = self.right[l, k]
        row = lax.broadcasted_iota(jnp.int32, right.shape, 0)
        return jnp.where(row < self.rank[0, l, 0, k], right, 0.0)

    def choose(self, l, k, low):
        slot = self.slot[0, l, 0, k]
        dense = self.dense[jnp.maximum(slot, 0)]
        return jnp.where(slot >= 0, dense, low)

    def tile(self, l, k):
        left = self.left[l, k]
        lh = left.astype(BF16).astype(F32)
        rh, rl = split(self.masked_right(l, k))
        zero = jnp.zeros_like(left)
        cols = jnp.concatenate([lh, left - lh, lh, zero], 0).T.astype(BF16)
        rows = jnp.concatenate([rh, rh, rl, zero.astype(BF16)], 0)
        return self.choose(l, k, dot_nn(cols, rows))

    def prepare_column(self, pair, half):
        k = 2 * pair + half
        blocks = self.left.shape[0]
        lt = jnp.concatenate([self.left[l, k] for l in range(blocks)], 0).T
        lh, ll = split(lt)
        rights = [split(self.masked_right(l, k)) for l in range(blocks)]

        def diagonal(part):
            zero = jnp.zeros_like(rights[0][0])
            return jnp.concatenate(
                [
                    jnp.concatenate([rights[l][part] if m == l else zero for m in range(blocks)], 1)
                    for l in range(blocks)
                ],
                0,
            )

        rh, rl = diagonal(0), diagonal(1)
        low = dot_nn(jnp.concatenate([lh, ll], 1), jnp.concatenate([rh, rh], 0)) + dot_nn(lh, rl)
        for l in range(blocks):
            th, tl = split(self.choose(l, k, low[:, 128 * l : 128 * (l + 1)]))
            self.wh[pair, 128 * l : 128 * (l + 1), 128 * half : 128 * (half + 1)] = th
            self.wl[pair, 128 * l : 128 * (l + 1), 128 * half : 128 * (half + 1)] = tl

    def prepare(self, pair):
        self.prepare_column(pair, 0)
        self.prepare_column(pair, 1)


class Leaf(Front):
    def partner(self, me):
        return me + 1 - 2 * lax.rem(me, 2)

    def side(self, me):
        return lax.rem(lax.rem(me, 4) + 1, 4) // 2

    def rows(self, side):
        return pl.ds(pl.multiple_of(side * self.half, self.half), self.half)

    def targets(self, me):
        odd = lax.rem(me, 2)
        for order, (to_even, to_odd) in enumerate(self.steps):
            yield order, lax.rem(me + to_even + (to_odd - to_even) * odd, self.tiles)

    def piece(self, pair, side, to, sem):
        part = self.x.at[pair, self.rows(side)]
        return pltpu.make_async_remote_copy(
            part, part, sem, self.xr.at[2 * pair + side],
            device_id={"tile": to}, device_id_type=MESH,
        )

    def send(self, source, target, sends, recvs, at, me):
        return pltpu.make_async_remote_copy(
            source, target, sends.at[at], recvs.at[at],
            device_id={"tile": self.partner(me)}, device_id_type=MESH,
        )

    def copy_d(self, l, me):
        return self.send(self.inverse.at[l], self.dother.at[l], self.ds, self.dr, l, me)

    def copy_t(self, l, me):
        return self.send(self.inner.at[l], self.inner.at[l], self.ts, self.tr, l, me)

    def copy_r(self, l, q, me):
        return pltpu.make_async_remote_copy(
            self.outer.at[l, q], self.outer.at[l, q], self.rs.at[l], self.rr.at[l],
            device_id={"tile": self.partner(me)}, device_id_type=MESH,
        )

    def copy_b(self, l, q, me):
        return pltpu.make_async_remote_copy(
            self.bout.at[l], self.bin.at[l, q], self.bs.at[l], self.br.at[l],
            device_id={"tile": self.partner(me)}, device_id_type=MESH,
        )

    def share_inner(self, l, me):
        self.copy_d(l, me).start()

        @pl.when(lax.rem(me, 2) == 1)
        def _():
            self.inner[l] = self.tile(l, 2 * (l * self.groups + me // 2))
            self.copy_t(l, me).start()

    def share_outer(self, l, me):
        prev = jnp.maximum(l * self.groups + me // 2 - 1, 0)
        q = lax.rem(me, 2)
        for half in range(2):
            self.outer[l, q, :, 128 * half : 128 * (half + 1)] = self.tile(l, 2 * prev + half)
        self.copy_r(l, q, me).start()

    def diagonals(self, l, me):
        even = lax.rem(me, 2) == 0
        mine, other = self.inverse[l], self.dother[l]
        return jnp.where(even, mine, other), jnp.where(even, other, mine)

    def make_g(self, l, me):
        self.copy_d(l, me).wait_recv()

        @pl.when(lax.rem(me, 2) == 0)
        def _():
            self.copy_t(l, me).wait_recv()

        first, second = self.diagonals(l, me)
        between = mul_nn(second, self.inner[l])
        self.bmat[l] = between
        zero = jnp.zeros((128, 128), BF16)
        low = split(-mul_nn(between, first))
        for ref, top, left, right in zip((self.gh, self.gl), split(first), low, split(second)):
            ref[l, :128, :128] = top
            ref[l, :128, 128:] = zero
            ref[l, 128:, :128] = left
            ref[l, 128:, 128:] = right

    def make_p(self, l, me):
        self.copy_r(l, 1 - lax.rem(me, 2), me).wait_recv()
        first, second = self.diagonals(l, me)
        top = mul_nn(first, self.outer[l, 0])
        bottom = mul_nn(second, self.outer[l, 1]) - mul_nn(self.bmat[l], top)
        self.ph[l, :128], self.pl[l, :128] = split(top)
        self.ph[l, 128:], self.pl[l, 128:] = split(bottom)

    def start_c(self, l, me):
        q, side = lax.rem(me, 2), self.side(me)
        self.bout[l] = self.b[l, self.rows(1 - side)]
        self.copy_b(l, q, me).start()
        self.bin[l, q] = self.b[l, self.rows(side)]

    def finish_c(self, l, me):
        self.copy_b(l, lax.rem(me, 2), me).wait_recv()
        whole = jnp.concatenate([self.bin[l, 0], self.bin[l, 1]], 1)
        self.c[l] = mul_nt(whole, self.gh[l], self.gl[l])

    def emit(self, l, me, solved):
        pair, side = l * self.groups + me // 2, self.side(me)
        self.x[pair, self.rows(side)] = solved
        for order, to in self.targets(me):
            self.piece(pair, side, to, self.xs.at[l, order]).start()

    def wait_piece(self, pair, side):
        self.piece(pair, side, 0, self.xs.at[0, 0]).wait_recv()

    def update(self, pair, me):
        out = mul_nt(self.x[pair], self.wh[pair], self.wl[pair])
        for l in range(self.b.shape[0]):
            part = out[:, 128 * l : 128 * (l + 1)]
            if l < 2:
                part = part * (l * self.groups + me // 2 > pair + 1).astype(F32)
            self.b[l] = self.b[l] - part

    def start(self, me):
        mine = me // 2
        self.share_inner(0, me)

        @pl.when(mine < 2)
        def _():
            self.start_c(0, me)

        self.share_outer(0, me)
        self.make_g(0, me)

        @pl.when(mine == 0)
        def _():
            self.finish_c(0, me)
            self.emit(0, me, self.c[0])

        self.make_p(0, me)

    def run(self, me, extra):
        pairs = 2 * self.groups
        mine, side = me // 2, self.side(me)

        def step(pair, carry):
            extra(pair)
            mine_next = jnp.logical_and(pair + 1 < pairs, mine == lax.rem(pair + 1, self.groups))
            mine_then = jnp.logical_and(pair + 2 < pairs, mine == lax.rem(pair + 2, self.groups))
            l_next = lax.rem(pair + 1, pairs) // self.groups
            l_then = lax.rem(pair + 2, pairs) // self.groups

            @pl.when(mine_next)
            def _():
                self.finish_c(l_next, me)

            @pl.when(mine != lax.rem(pair, self.groups))
            def _():
                self.wait_piece(pair, side)

            @pl.when(mine_next)
            def _():
                solved = mul_nt(self.x[pair, self.rows(side)], self.ph[l_next], self.pl[l_next])
                self.emit(l_next, me, self.c[l_next] - solved)

            self.wait_piece(pair, 1 - side)
            self.update(pair, me)

            @pl.when(mine_then)
            def _():
                self.start_c(l_then, me)

            return carry

        lax.fori_loop(0, pairs, step, 0)

    def write(self, me, pivots):
        for l in range(2):
            for other in range(2):
                @pl.when(lax.rem(me, 2) == other)
                def _(l=l, other=other):
                    pivots[l] = self.x[l * self.groups + me // 2, :, 128 * other : 128 * (other + 1)]

    def wait_sends(self, me):
        q, side = lax.rem(me, 2), self.side(me)
        for l in range(2):
            for order, to in self.targets(me):
                self.piece(l * self.groups + me // 2, side, to, self.xs.at[l, order]).wait_send()
            self.copy_d(l, me).wait_send()
            self.copy_r(l, q, me).wait_send()
            self.copy_b(l, q, me).wait_send()

            @pl.when(q == 1)
            def _(l=l):
                self.copy_t(l, me).wait_send()


SPAN = 4


class Root(Front):
    def place(self, me):
        return me // SPAN, lax.rem(me, SPAN)

    def beside(self, me, step):
        y, q = self.place(me)
        return y * SPAN + lax.rem(q + step, SPAN)

    def z_tile(self, l, q, to, step):
        return pltpu.make_async_remote_copy(
            self.zall.at[l, self.my_leaf, q], self.zall.at[l, self.my_leaf, q],
            self.zs.at[l, step], self.zr.at[l, q],
            device_id={"tile": to}, device_id_type=MESH,
        )

    def z_leaf(self, l, which, there, sends, step):
        return pltpu.make_async_remote_copy(
            self.zall.at[l, which], self.zall.at[l, which], sends.at[l, step], self.gr.at[l, which],
            device_id={"leaf": there}, device_id_type=MESH,
        )

    def partner(self):
        return self.my_leaf + 1 - 2 * lax.rem(self.my_leaf, 2)

    def solve_z(self, l, me):
        y, q = self.place(me)
        group = l * self.groups + y
        column = SPAN * jnp.maximum(group - 1, 0) + jnp.minimum(self.my_leaf, SPAN - 1)
        shape = (128, 128)
        same = lax.broadcasted_iota(jnp.int32, shape, 0) == lax.broadcasted_iota(jnp.int32, shape, 1)
        unit = same.astype(F32) * (self.my_leaf - SPAN == q).astype(F32)
        self.zwork[...] = jnp.where(self.my_leaf < SPAN, self.tile(l, column), unit)
        for before in range(SPAN - 1):
            @pl.when(before < q)
            def _(before=before):
                inner = self.tile(l, SPAN * group + before)
                self.z_tile(l, before, me, 0).wait_recv()
                known = self.zall[l, self.my_leaf, before]
                self.zwork[...] = self.zwork[...] - mul_nn(inner, known)

        self.zall[l, self.my_leaf, q] = mul_nn(self.inverse[l], self.zwork[...])
        for step in range(1, SPAN):
            self.z_tile(l, q, self.beside(me, step), step).start()

    def send_over_x(self, l, me):
        q = lax.rem(me, SPAN)
        for after in range(1, SPAN):
            @pl.when(after > q)
            def _(after=after):
                self.z_tile(l, after, me, 0).wait_recv()

        for step in range(2, self.leaves, 2):
            there = lax.rem(self.my_leaf + step, self.leaves)
            self.z_leaf(l, self.my_leaf, there, self.gs, step).start()

    def send_to_core(self, l):
        for step in range(0, self.leaves, 2):
            which = lax.rem(self.my_leaf + step, self.leaves)
            if step:
                self.z_leaf(l, which, which, self.gs, step).wait_recv()
            self.z_leaf(l, which, self.partner(), self.ks, step).start()

    def take_z(self, l):
        for step in range(0, self.leaves, 2):
            which = lax.rem(self.partner() + step, self.leaves)
            self.z_leaf(l, which, which, self.ks, step).wait_recv()
        for g in range(2 * SPAN):
            at = slice(128 * (g % SPAN), 128 * (g % SPAN + 1))
            for q in range(SPAN):
                row = slice(128 * q, 128 * (q + 1))
                if g < SPAN:
                    self.ph[l, row, at], self.pl[l, row, at] = split(self.zall[l, g, q])
                else:
                    self.gh[l, row, at], self.gl[l, row, at] = split(self.zall[l, g, q])

    def send_group(self, l, me, down):
        y, q = self.place(me)
        group = l * self.groups + y
        to = lax.rem(y + down, self.groups) * SPAN + q
        return pltpu.make_async_remote_copy(
            self.x.at[group], self.x.at[group], self.xs.at[l, down], self.xr.at[group],
            device_id={"tile": to}, device_id_type=MESH,
        )

    def emit(self, l, me, solved):
        self.x[l * self.groups + me // SPAN] = solved
        for down in range(1, self.groups):
            self.send_group(l, me, down).start()

    def arrive(self, group, me):
        @pl.when(me // SPAN != lax.rem(group, self.groups))
        def _():
            pltpu.make_async_remote_copy(
                self.x.at[group], self.x.at[group], self.xs.at[0, 0], self.xr.at[group],
                device_id={"tile": 0}, device_id_type=MESH,
            ).wait_recv()

    def copy_b(self, l, q, to, step):
        return pltpu.make_async_remote_copy(
            self.bin.at[l, q], self.bin.at[l, q], self.bs.at[l, step], self.br.at[l, q],
            device_id={"tile": to}, device_id_type=MESH,
        )

    def start_c(self, l, me):
        q = lax.rem(me, SPAN)
        self.bin[l, q] = self.b[l]
        for step in (2, 1, 3):
            self.copy_b(l, q, self.beside(me, step), step).start()

    def finish_c(self, l, me):
        for step in (1, 3, 2):
            q = lax.rem(me + step, SPAN)
            self.copy_b(l, q, me, 0).wait_recv()
        whole = jnp.concatenate([self.bin[l, other] for other in range(SPAN)], 1)
        self.c[l] = mul_nt(whole, self.gh[l], self.gl[l])

    def update(self, group, me):
        now = self.x[group]
        out = mul_nt(now[:, :256], self.wh[2 * group], self.wl[2 * group])
        out = out + mul_nt(now[:, 256:], self.wh[2 * group + 1], self.wl[2 * group + 1])
        for l in range(self.b.shape[0]):
            part = out[:, 128 * l : 128 * (l + 1)]
            if l < 2:
                part = part * (l * self.groups + me // SPAN > group + 1).astype(F32)
            self.b[l] = self.b[l] - part

    def run(self, me):
        groups = 2 * self.groups
        y = me // SPAN

        @pl.when(y < 2)
        def _():
            self.start_c(0, me)

        @pl.when(y == 0)
        def _():
            self.finish_c(0, me)
            self.emit(0, me, self.c[0])

        def step(group, carry):
            mine_next = jnp.logical_and(group + 1 < groups, y == lax.rem(group + 1, self.groups))
            mine_then = jnp.logical_and(group + 2 < groups, y == lax.rem(group + 2, self.groups))
            l_next = lax.rem(group + 1, groups) // self.groups
            l_then = lax.rem(group + 2, groups) // self.groups

            @pl.when(mine_next)
            def _():
                self.finish_c(l_next, me)

            self.arrive(group, me)

            @pl.when(mine_next)
            def _():
                solved = mul_nt(self.x[group], self.ph[l_next], self.pl[l_next])
                self.emit(l_next, me, self.c[l_next] - solved)

            self.update(group, me)

            @pl.when(group == 0)
            def _():
                self.send_to_core(1)

            @pl.when(group == 1)
            def _():
                self.take_z(1)

            @pl.when(mine_then)
            def _():
                self.start_c(l_then, me)

            return carry

        lax.fori_loop(0, groups, step, 0)

    def write(self, me, pivots):
        y, q = self.place(me)
        for l in range(2):
            for other in range(SPAN):
                @pl.when(other == q)
                def _(l=l, other=other):
                    pivots[l] = self.x[l * self.groups + y, :, 128 * other : 128 * (other + 1)]

    def wait_sends(self, me):
        q = lax.rem(me, SPAN)
        for l in range(2):
            for down in range(1, self.groups):
                self.send_group(l, me, down).wait_send()
            for step in range(1, SPAN):
                self.copy_b(l, q, self.beside(me, step), step).wait_send()
                self.z_tile(l, q, self.beside(me, step), step).wait_send()
            for step in range(0, self.leaves, 2):
                which = lax.rem(self.my_leaf + step, self.leaves)
                if step:
                    self.z_leaf(l, self.my_leaf, which, self.gs, step).wait_send()
                self.z_leaf(l, which, self.partner(), self.ks, step).wait_send()


def kernel(sizes, *refs):
    tiles, leaves, blocks, sources = sizes
    share = sources // leaves
    names_in = ("forcing", "inverse", "dense", "slot", "left", "right", "rank")
    leaf_in = dict(zip(names_in, refs[:7]))
    place = refs[7]
    root_in = dict(zip(names_in, refs[8:15]))
    leaf_pivots, root_pivots, root_updates = refs[15:18]
    scratch = list(refs[18:])
    me = lax.axis_index("tile")
    my_leaf = lax.axis_index("leaf")
    even_steps, odd_steps = [3, 4, 5, 2, 1], [1, 4, 3, 2, tiles - 1]
    for steps in (even_steps, odd_steps):
        steps[:] = list(dict.fromkeys(s for s in steps + list(range(1, tiles)) if 0 < s < tiles))
    order = list(zip(even_steps, odd_steps))

    common = (
        "b", "x", "c", "wh", "wl", "inverse", "dense", "left", "right", "xs", "xr", "load", "ph", "pl",
    )
    for_leaf = (
        "gh", "gl", "bin", "bout", "dother", "inner", "outer", "bmat",
        "ds", "dr", "ts", "tr", "rs", "rr", "bs", "br",
    )
    for_root = (
        "gh", "gl", "bin", "zall", "zwork", "zs", "zr", "gs", "ks", "gr", "bs", "br",
    )

    def front_of(kind, inputs, names, groups, **more):
        mine = {name: scratch.pop(0) for name in names}
        return kind(
            slot=inputs["slot"], rank=inputs["rank"], tiles=tiles, groups=groups, **more, **mine
        )

    leaf = front_of(
        Leaf, leaf_in, common + for_leaf, tiles // 2, steps=order, half=sources // 2
    )
    root = front_of(
        Root, root_in, common + for_root, tiles // SPAN, leaves=leaves, my_leaf=my_leaf
    )
    root_forcing, sum_out, sum_in, sum_send, sum_recv = scratch

    def load(front, inputs, forcing):
        pairs = [(inputs["forcing"], forcing)] + [
            (inputs[n], getattr(front, n)) for n in ("inverse", "left", "right", "dense")
        ]
        return [
            pltpu.make_async_copy(src, dst, front.load.at[n]) for n, (src, dst) in enumerate(pairs)
        ]

    leaf_loads = load(leaf, leaf_in, leaf.b)
    root_loads = load(root, root_in, root_forcing)
    for copy in leaf_loads:
        copy.start()
    for copy in root_loads:
        copy.start()

    barrier = pltpu.get_barrier_semaphore()
    for step in range(1, tiles):
        pl.semaphore_signal(
            barrier, inc=1, device_id={"tile": lax.rem(me + step, tiles)}, device_id_type=MESH
        )
    for step in range(1, leaves):
        pl.semaphore_signal(
            barrier, inc=1, device_id={"leaf": lax.rem(my_leaf + step, leaves)}, device_id_type=MESH
        )
    for copy in leaf_loads:
        copy.wait()
    pl.semaphore_wait(barrier, tiles + leaves - 2)

    leaf.start(me)
    for copy in root_loads:
        copy.wait()

    def beside(pair):
        leaf.prepare(pair)
        root.prepare(pair)

        @pl.when(pair == 1)
        def _():
            leaf.share_inner(1, me)
            leaf.share_outer(1, me)

        @pl.when(pair == SPAN + 1)
        def _():
            leaf.make_g(1, me)
            leaf.make_p(1, me)


        y, q = root.place(me)

        @pl.when(pair == 1 + 2 * q)
        def _():
            root.solve_z(0, me)

        @pl.when(pair == 3 + 2 * q + 2)
        def _():
            root.solve_z(1, me)

        @pl.when(pair == 9)
        def _():
            root.send_over_x(0, me)

        @pl.when(pair == 13)
        def _():
            root.send_over_x(1, me)

        @pl.when(pair == 15)
        def _():
            root.send_to_core(0)

    leaf.run(me, beside)

    leaf.write(me, leaf_pivots)

    for m in range(blocks):
        part = jnp.zeros((sources, 128), F32)
        for u in range(2):
            part = part + leaf.b[2 + u] * (place[0, 0, u] == m).astype(F32)
        for g in range(leaves):
            sum_out[g, m] = part[share * g : share * (g + 1)]

    def sum_copy(step, there):
        return pltpu.make_async_remote_copy(
            sum_out.at[there], sum_in.at[my_leaf], sum_send.at[step], sum_recv.at[my_leaf],
            device_id={"leaf": there}, device_id_type=MESH,
        )

    def sum_wait(here):
        return pltpu.make_async_remote_copy(
            sum_out.at[here], sum_in.at[here], sum_send.at[0], sum_recv.at[here],
            device_id={"leaf": here}, device_id_type=MESH,
        )

    for step in range(1, leaves):
        sum_copy(step, lax.rem(my_leaf + step, leaves)).start()
    for m in range(blocks):
        mine = root_forcing[m, pl.ds(pl.multiple_of(my_leaf * share, share), share)]
        root.b[m] = mine + sum_out[my_leaf, m]
    root.take_z(0)
    for step in range(1, leaves):
        here = lax.rem(my_leaf + step, leaves)
        sum_wait(here).wait_recv()
        for m in range(blocks):
            root.b[m] = root.b[m] + sum_in[here, m]

    root.run(me)
    root.write(me, root_pivots)
    for l in range(2):
        root_updates[l] = root.b[2 + l]

    leaf.wait_sends(me)
    root.wait_sends(me)
    for step in range(1, leaves):
        sum_copy(step, lax.rem(my_leaf + step, leaves)).wait_send()


def common_scratch(tiles, blocks, sources, dense_count, rank, x, c, p):
    pivots = 2 * tiles
    blk = 128
    vmem = pltpu.VMEM
    dma = pltpu.SemaphoreType.DMA
    return [
        vmem((blocks, sources, blk), F32),
        vmem(x, F32),
        vmem(c, F32),
        vmem((tiles, blocks * blk, 2 * blk), BF16),
        vmem((tiles, blocks * blk, 2 * blk), BF16),
        vmem((2, blk, blk), F32),
        vmem((dense_count, blk, blk), F32),
        vmem((blocks, pivots, rank, blk), F32),
        vmem((blocks, pivots, rank, blk), F32),
        dma((2, tiles)),
        dma((pivots,)),
        dma((5,)),
        vmem(p, BF16),
        vmem(p, BF16),
    ]


def leaf_scratch(sources):
    blk = 128
    vmem = pltpu.VMEM
    dma = pltpu.SemaphoreType.DMA
    return [
        vmem((2, 2 * blk, 2 * blk), BF16),
        vmem((2, 2 * blk, 2 * blk), BF16),
        vmem((2, 2, sources // 2, blk), F32),
        vmem((2, sources // 2, blk), F32),
        vmem((2, blk, blk), F32),
        vmem((2, blk, blk), F32),
        vmem((2, 2, blk, 2 * blk), F32),
        vmem((2, blk, blk), F32),
    ] + [dma((2,))] * 8


def root_scratch(sources, leaves):
    blk = 128
    vmem = pltpu.VMEM
    dma = pltpu.SemaphoreType.DMA
    return [
        vmem((2, SPAN * blk, SPAN * blk), BF16),
        vmem((2, SPAN * blk, SPAN * blk), BF16),
        vmem((2, SPAN, sources, blk), F32),
        vmem((2, leaves, SPAN, blk, blk), F32),
        vmem((blk, blk), F32),
        dma((2, SPAN)),
        dma((2, SPAN)),
        dma((2, leaves)),
        dma((2, leaves)),
        dma((2, leaves)),
        dma((2, SPAN)),
        dma((2, SPAN)),
    ]


def hand_over(*refs):
    for source, result in zip(refs[:3], refs[3:]):
        result[...] = source[...]


def body(
    forcing_leaf,
    inverse_leaf,
    dense_leaf,
    slot_leaf,
    left_leaf,
    right_leaf,
    rank_leaf,
    place_leaf,
    forcing_root,
    inverse_root,
    dense_root,
    slot_root,
    left_root,
    right_root,
    rank_root,
):
    tiles = lax.axis_size("tile")
    leaves = lax.axis_size("leaf")
    blocks, sources, blk = forcing_leaf.shape[1], forcing_leaf.shape[3], forcing_leaf.shape[4]
    dense_count, rank = dense_leaf.shape[2], left_leaf.shape[4]
    share = sources // leaves
    args = (
        forcing_leaf[0, :, 0],
        inverse_leaf[0, :, 0],
        dense_leaf[0, 0],
        slot_leaf,
        left_leaf[0, :, 0],
        right_leaf[0, :, 0],
        rank_leaf,
        place_leaf.transpose(0, 2, 1),
        forcing_root[:, 0],
        inverse_root[:, 0],
        dense_root[0],
        slot_root[None],
        left_root[:, 0],
        right_root[:, 0],
        rank_root[None],
    )
    smem = pl.BlockSpec(memory_space=pltpu.SMEM)
    hbm = pl.BlockSpec(memory_space=pl.ANY)
    vmem = pl.BlockSpec(memory_space=pltpu.VMEM)
    one = [hbm, hbm, hbm, smem, hbm, hbm, smem]
    shapes = (
        jax.ShapeDtypeStruct((2, sources, blk), F32),
        jax.ShapeDtypeStruct((2, share, blk), F32),
        jax.ShapeDtypeStruct((2, share, blk), F32),
    )
    solved = pl.pallas_call(
        functools.partial(kernel, (tiles, leaves, blocks, sources)),
        out_shape=shapes,
        in_specs=one + [smem] + one,
        out_specs=(vmem, vmem, vmem),
        scratch_shapes=common_scratch(
            tiles, blocks, sources, dense_count, rank,
            (tiles, sources, 2 * blk), (2, sources // 2, 2 * blk), (2, 2 * blk, 2 * blk),
        )
        + leaf_scratch(sources)
        + common_scratch(
            tiles, blocks, share, dense_count, rank,
            (2 * tiles // SPAN, share, SPAN * blk), (2, share, SPAN * blk), (2, SPAN * blk, SPAN * blk),
        )
        + root_scratch(share, leaves)
        + [
            pltpu.VMEM((blocks, sources, blk), F32),
            pltpu.VMEM((leaves, blocks, share, blk), F32),
            pltpu.VMEM((leaves, blocks, share, blk), F32),
            pltpu.SemaphoreType.DMA((leaves,)),
            pltpu.SemaphoreType.DMA((leaves,)),
        ],
        compiler_params=pltpu.CompilerParams(
            collective_id=0, has_side_effects=True, vmem_limit_bytes=60 * 2**20
        ),
    )(*args)
    leaf_pivots, root_pivots, root_updates = pl.pallas_call(
        hand_over, out_shape=shapes, in_specs=[vmem] * 3, out_specs=(vmem, vmem, vmem)
    )(*solved)
    return leaf_pivots[None, :, None], root_pivots[:, None], root_updates[:, None]


def solution(mesh):
    placed = (
        P("leaf", None, "tile", None, None),
        P("leaf", None, "tile", None, None),
        P("leaf", "tile", None, None, None),
        P("leaf", None, "tile", None),
        P("leaf", None, "tile", None, None, None),
        P("leaf", None, "tile", None, None, None),
        P("leaf", None, "tile", None),
        P("leaf", None, "tile"),
        P(None, "tile", None, None),
        P(None, "tile", None, None),
        P("tile", None, None, None),
        P(None, "tile", None),
        P(None, "tile", None, None, None),
        P(None, "tile", None, None, None),
        P(None, "tile", None),
    )
    return jax.shard_map(
        body,
        mesh=mesh,
        in_specs=placed,
        out_specs=(
            P("leaf", None, "tile", None, None),
            P(None, "tile", "leaf", None),
            P(None, "tile", "leaf", None),
        ),
        check_vma=False,
    )
```

time: 137 us -> 126 us (0.920)
  Pallas kernels: 131 us -> 125 us
  local copies, waits for them, and re-layouts: 5.36 us -> 0 us
    pallas_call x1, Pallas kernels: 131 us -> 124 us  [body(): pl.pallas_call(functools.partial(kernel, (tiles, leaves, blocks, sources)...]
    unnamed x4 -> x0, local copies, waits for them, and re-layouts: 5.36 us -> none
    pallas_call x0 -> x1, Pallas kernels: none -> 1.5 us  [body(): pl.pallas_call(hand_over, out_shape=shapes, in_specs=[vmem] * 3, out_spec...]
where the time goes in v3:
time: 126 us
  Pallas kernels  125 us (99%)
    pallas_call x1, Pallas kernels, body(): pl.pallas_call(functools.partial(kernel, (tiles, leaves, blocks, sources)...  124 us

profile of v3, /device:TPU:0, one launch (start us, length us, event | category | flops | bytes accessed | tf_op | source)
XLA Modules:
  0.0 126.1 jit_solution(14979238122912778227)
XLA Ops:
  0.6 123.9 %shard_map.166 = (f32[2,64,128]{2,1,0:T(8,128)}, f32[2,8,128]{2,1,0:T(8,128)}, f32[2,8,128]{2,1,0:T(8,128)}) custom-call(f32[4,64,128]{2,1,0:T(8,128)} %bitcast.32, f32[2,128,128]{2,1,0:T(8,128)} %bitcast.33, f32[32,128,128]{2,1,0:T(8,128)} %bitcast.26, s32[1,4,1,32]{3,2,1,0:T(1,128)} %refs_3_.1, f32[4,32,32,128]{3,2,1,0:T(8,128)} %bitcast.27, ...), custom_call_target="tpu_custom_call" | custom-call | tf_op jit(solution)/shard_map/pallas_call | solution.py:757
  124.6 1.5 %shard_map.167 = (f32[2,64,128]{2,1,0:T(8,128)}, f32[2,8,128]{2,1,0:T(8,128)}, f32[2,8,128]{2,1,0:T(8,128)}) custom-call(f32[2,64,128]{2,1,0:T(8,128)} %get-tuple-element.9.refs_0_, f32[2,8,128]{2,1,0:T(8,128)} %get-tuple-element.10.refs_1_, f32[2,8,128]{2,1,0:T(8,128)} %get-tuple-element.11.refs_2_), custom_call_target="tpu_custom_call" | custom-call | tf_op jit(solution)/shard_map/pallas_call | solution.py:783

commit v4 on v3

--- a/solution.py
+++ b/solution.py
@@ -297,72 +297,103 @@
         y, q = self.place(me)
         return y * SPAN + lax.rem(q + step, SPAN)
 
-    def z_tile(self, l, q, to, step):
-        return pltpu.make_async_remote_copy(
-            self.zall.at[l, self.my_leaf, q], self.zall.at[l, self.my_leaf, q],
-            self.zs.at[l, step], self.zr.at[l, q],
+    def z_slot(self, which):
+        return 2 * SPAN + self.my_leaf // 2 if which else self.my_leaf
+
+    def z_tile(self, l, which, q, to, step):
+        part = self.zall.at[l, self.z_slot(which), q]
+        return pltpu.make_async_remote_copy(
+            part, part, self.zs.at[2 * l + which, step], self.zr.at[2 * l + which, q],
             device_id={"tile": to}, device_id_type=MESH,
         )
 
-    def z_leaf(self, l, which, there, sends, step):
-        return pltpu.make_async_remote_copy(
-            self.zall.at[l, which], self.zall.at[l, which], sends.at[l, step], self.gr.at[l, which],
+    def z_leaf(self, l, which, owner, there, sends, step):
+        slot = 2 * SPAN + owner // 2 if which else owner
+        part = self.zall.at[l, slot]
+        return pltpu.make_async_remote_copy(
+            part, part, sends.at[2 * l + which, step], self.gr.at[l, slot],
             device_id={"leaf": there}, device_id_type=MESH,
         )
 
     def partner(self):
         return self.my_leaf + 1 - 2 * lax.rem(self.my_leaf, 2)
+
+    def parts(self, owner, do):
+        do(0)
+
+        @pl.when(lax.rem(owner, 2) == 0)
+        def _():
+            do(1)
 
     def solve_z(self, l, me):
         y, q = self.place(me)
         group = l * self.groups + y
-        column = SPAN * jnp.maximum(group - 1, 0) + jnp.minimum(self.my_leaf, SPAN - 1)
-        shape = (128, 128)
-        same = lax.broadcasted_iota(jnp.int32, shape, 0) == lax.broadcasted_iota(jnp.int32, shape, 1)
-        unit = same.astype(F32) * (self.my_leaf - SPAN == q).astype(F32)
-        self.zwork[...] = jnp.where(self.my_leaf < SPAN, self.tile(l, column), unit)
-        for before in range(SPAN - 1):
-            @pl.when(before < q)
-            def _(before=before):
-                inner = self.tile(l, SPAN * group + before)
-                self.z_tile(l, before, me, 0).wait_recv()
-                known = self.zall[l, self.my_leaf, before]
-                self.zwork[...] = self.zwork[...] - mul_nn(inner, known)
-
-        self.zall[l, self.my_leaf, q] = mul_nn(self.inverse[l], self.zwork[...])
-        for step in range(1, SPAN):
-            self.z_tile(l, q, self.beside(me, step), step).start()
+
+        def one(which):
+            block = self.my_leaf // 2 if which else jnp.minimum(self.my_leaf, SPAN - 1)
+            column = SPAN * jnp.maximum(group - 1 - which, 0) + block
+            start = self.tile(l, column)
+            if which == 0:
+                shape = (128, 128)
+                down = lax.broadcasted_iota(jnp.int32, shape, 0)
+                right = lax.broadcasted_iota(jnp.int32, shape, 1)
+                unit = (down == right).astype(F32) * (self.my_leaf - SPAN == q).astype(F32)
+                start = jnp.where(self.my_leaf < SPAN, start, unit)
+            self.zwork[...] = start
+            for before in range(SPAN - 1):
+                @pl.when(before < q)
+                def _(before=before):
+                    inner = self.tile(l, SPAN * group + before)
+                    self.z_tile(l, which, before, me, 0).wait_recv()
+                    known = self.zall[l, self.z_slot(which), before]
+                    self.zwork[...] = self.zwork[...] - mul_nn(inner, known)
+
+            self.zall[l, self.z_slot(which), q] = mul_nn(self.inverse[l], self.zwork[...])
+            for step in range(1, SPAN):
+                self.z_tile(l, which, q, self.beside(me, step), step).start()
+
+        self.parts(self.my_leaf, one)
 
     def send_over_x(self, l, me):
         q = lax.rem(me, SPAN)
-        for after in range(1, SPAN):
-            @pl.when(after > q)
-            def _(after=after):
-                self.z_tile(l, after, me, 0).wait_recv()
-
-        for step in range(2, self.leaves, 2):
-            there = lax.rem(self.my_leaf + step, self.leaves)
-            self.z_leaf(l, self.my_leaf, there, self.gs, step).start()
+
+        def one(which):
+            for after in range(1, SPAN):
+                @pl.when(after > q)
+                def _(after=after):
+                    self.z_tile(l, which, after, me, 0).wait_recv()
+
+            for step in range(2, self.leaves, 2):
+                there = lax.rem(self.my_leaf + step, self.leaves)
+                self.z_leaf(l, which, self.my_leaf, there, self.gs, step).start()
+
+        self.parts(self.my_leaf, one)
 
     def send_to_core(self, l):
         for step in range(0, self.leaves, 2):
-            which = lax.rem(self.my_leaf + step, self.leaves)
-            if step:
-                self.z_leaf(l, which, which, self.gs, step).wait_recv()
-            self.z_leaf(l, which, self.partner(), self.ks, step).start()
+            owner = lax.rem(self.my_leaf + step, self.leaves)
+
+            def one(which, step=step, owner=owner):
+                if step:
+                    self.z_leaf(l, which, owner, owner, self.gs, step).wait_recv()
+                self.z_leaf(l, which, owner, self.partner(), self.ks, step).start()
+
+            self.parts(owner, one)
 
     def take_z(self, l):
         for step in range(0, self.leaves, 2):
-            which = lax.rem(self.partner() + step, self.leaves)
-            self.z_leaf(l, which, which, self.ks, step).wait_recv()
-        for g in range(2 * SPAN):
+            owner = lax.rem(self.partner() + step, self.leaves)
+
+            def one(which, step=step, owner=owner):
+                self.z_leaf(l, which, owner, owner, self.ks, step).wait_recv()
+
+            self.parts(owner, one)
+        for g in range(3 * SPAN):
             at = slice(128 * (g % SPAN), 128 * (g % SPAN + 1))
+            high, low = ((self.ph, self.pl), (self.gh, self.gl), (self.fh, self.fl))[g // SPAN]
             for q in range(SPAN):
                 row = slice(128 * q, 128 * (q + 1))
-                if g < SPAN:
-                    self.ph[l, row, at], self.pl[l, row, at] = split(self.zall[l, g, q])
-                else:
-                    self.gh[l, row, at], self.gl[l, row, at] = split(self.zall[l, g, q])
+                high[l, row, at], low[l, row, at] = split(self.zall[l, g, q])
 
     def send_group(self, l, me, down):
         y, q = self.place(me)
@@ -412,32 +443,33 @@
         for l in range(self.b.shape[0]):
             part = out[:, 128 * l : 128 * (l + 1)]
             if l < 2:
-                part = part * (l * self.groups + me // SPAN > group + 1).astype(F32)
+                part = part * (l * self.groups + me // SPAN > group + 2).astype(F32)
             self.b[l] = self.b[l] - part
 
     def run(self, me):
         groups = 2 * self.groups
         y = me // SPAN
 
+        @pl.when(y < 3)
+        def _():
+            self.start_c(0, me)
+
         @pl.when(y < 2)
         def _():
-            self.start_c(0, me)
+            self.finish_c(0, me)
 
         @pl.when(y == 0)
         def _():
-            self.finish_c(0, me)
             self.emit(0, me, self.c[0])
 
         def step(group, carry):
-            mine_next = jnp.logical_and(group + 1 < groups, y == lax.rem(group + 1, self.groups))
-            mine_then = jnp.logical_and(group + 2 < groups, y == lax.rem(group + 2, self.groups))
-            l_next = lax.rem(group + 1, groups) // self.groups
-            l_then = lax.rem(group + 2, groups) // self.groups
-
-            @pl.when(mine_next)
-            def _():
-                self.finish_c(l_next, me)
-
+            def mine(ahead):
+                here = jnp.logical_and(group + ahead < groups, y == lax.rem(group + ahead, self.groups))
+                return here, lax.rem(group + ahead, groups) // self.groups
+
+            mine_next, l_next = mine(1)
+            mine_then, l_then = mine(2)
+            mine_late, l_late = mine(3)
             self.arrive(group, me)
 
             @pl.when(mine_next)
@@ -447,17 +479,22 @@
 
             self.update(group, me)
 
+            @pl.when(mine_late)
+            def _():
+                self.start_c(l_late, me)
+
             @pl.when(group == 0)
             def _():
                 self.send_to_core(1)
 
-            @pl.when(group == 1)
+            @pl.when(group == 2)
             def _():
                 self.take_z(1)
 
             @pl.when(mine_then)
             def _():
-                self.start_c(l_then, me)
+                self.finish_c(l_then, me)
+                self.c[l_then] = self.c[l_then] - mul_nt(self.x[group], self.fh[l_then], self.fl[l_then])
 
             return carry
 
@@ -478,12 +515,22 @@
                 self.send_group(l, me, down).wait_send()
             for step in range(1, SPAN):
                 self.copy_b(l, q, self.beside(me, step), step).wait_send()
-                self.z_tile(l, q, self.beside(me, step), step).wait_send()
+
+            def own(which, l=l):
+                for step in range(1, SPAN):
+                    self.z_tile(l, which, q, self.beside(me, step), step).wait_send()
+                for step in range(2, self.leaves, 2):
+                    there = lax.rem(self.my_leaf + step, self.leaves)
+                    self.z_leaf(l, which, self.my_leaf, there, self.gs, step).wait_send()
+
+            self.parts(self.my_leaf, own)
             for step in range(0, self.leaves, 2):
-                which = lax.rem(self.my_leaf + step, self.leaves)
-                if step:
-                    self.z_leaf(l, self.my_leaf, which, self.gs, step).wait_send()
-                self.z_leaf(l, which, self.partner(), self.ks, step).wait_send()
+                owner = lax.rem(self.my_leaf + step, self.leaves)
+
+                def passed(which, l=l, step=step, owner=owner):
+                    self.z_leaf(l, which, owner, self.partner(), self.ks, step).wait_send()
+
+                self.parts(owner, passed)
 
 
 def kernel(sizes, *refs):
@@ -510,7 +557,7 @@
         "ds", "dr", "ts", "tr", "rs", "rr", "bs", "br",
     )
     for_root = (
-        "gh", "gl", "bin", "zall", "zwork", "zs", "zr", "gs", "ks", "gr", "bs", "br",
+        "gh", "gl", "fh", "fl", "bin", "zall", "zwork", "zs", "zr", "gs", "ks", "gr", "bs", "br",
     )
 
     def front_of(kind, inputs, names, groups, **more):
@@ -574,13 +621,13 @@
             leaf.make_p(1, me)
 
 
-        y, q = root.place(me)
-
-        @pl.when(pair == 1 + 2 * q)
+        q = lax.rem(me, SPAN)
+
+        @pl.when(pair == 2 + 2 * q)
         def _():
             root.solve_z(0, me)
 
-        @pl.when(pair == 3 + 2 * q + 2)
+        @pl.when(pair == 3 + 2 * q)
         def _():
             root.solve_z(1, me)
 
@@ -588,7 +635,7 @@
         def _():
             root.send_over_x(0, me)
 
-        @pl.when(pair == 13)
+        @pl.when(pair == 10)
         def _():
             root.send_over_x(1, me)
 
@@ -685,17 +732,15 @@
     blk = 128
     vmem = pltpu.VMEM
     dma = pltpu.SemaphoreType.DMA
-    return [
-        vmem((2, SPAN * blk, SPAN * blk), BF16),
-        vmem((2, SPAN * blk, SPAN * blk), BF16),
+    return [vmem((2, SPAN * blk, SPAN * blk), BF16)] * 4 + [
         vmem((2, SPAN, sources, blk), F32),
-        vmem((2, leaves, SPAN, blk, blk), F32),
+        vmem((2, 3 * SPAN, SPAN, blk, blk), F32),
         vmem((blk, blk), F32),
-        dma((2, SPAN)),
-        dma((2, SPAN)),
-        dma((2, leaves)),
-        dma((2, leaves)),
-        dma((2, leaves)),
+        dma((4, SPAN)),
+        dma((4, SPAN)),
+        dma((4, leaves)),
+        dma((4, leaves)),
+        dma((2, 3 * SPAN)),
         dma((2, SPAN)),
         dma((2, SPAN)),
     ]

time: 126 us -> 126 us (level)
  no operation moved by 1% of the time
where the time goes in v4:
time: 126 us; the launch traced here: 125 us
  Pallas kernels  125 us (99%)
    pallas_call x1, Pallas kernels, body(): pl.pallas_call(functools.partial(kernel, (tiles, leaves, blocks, sources)...  123 us

profile of v4, /device:TPU:0, one launch (start us, length us, event | category | flops | bytes accessed | tf_op | source)
XLA Modules:
  0.0 125.4 jit_solution(16501183338644308217)
XLA Ops:
  0.6 123.3 %shard_map.166 = (f32[2,64,128]{2,1,0:T(8,128)}, f32[2,8,128]{2,1,0:T(8,128)}, f32[2,8,128]{2,1,0:T(8,128)}) custom-call(f32[4,64,128]{2,1,0:T(8,128)} %bitcast.32, f32[2,128,128]{2,1,0:T(8,128)} %bitcast.33, f32[32,128,128]{2,1,0:T(8,128)} %bitcast.26, s32[1,4,1,32]{3,2,1,0:T(1,128)} %refs_3_.1, f32[4,32,32,128]{3,2,1,0:T(8,128)} %bitcast.27, ...), custom_call_target="tpu_custom_call" | custom-call | tf_op jit(solution)/shard_map/pallas_call | solution.py:802
  123.9 1.5 %shard_map.167 = (f32[2,64,128]{2,1,0:T(8,128)}, f32[2,8,128]{2,1,0:T(8,128)}, f32[2,8,128]{2,1,0:T(8,128)}) custom-call(f32[2,64,128]{2,1,0:T(8,128)} %get-tuple-element.9.refs_0_, f32[2,8,128]{2,1,0:T(8,128)} %get-tuple-element.10.refs_1_, f32[2,8,128]{2,1,0:T(8,128)} %get-tuple-element.11.refs_2_), custom_call_target="tpu_custom_call" | custom-call | tf_op jit(solution)/shard_map/pallas_call | solution.py:828
